TPU v7x, 768 devices: a whole 4x8x12 slice. The times are simulated.
768 devices in a mesh: row: 32 (over y_lo, x, core), col: 24 (over y_hi, z).
Axes of the slice: x: 4, y: 8 (y_hi: 2, y_lo: 4; y = y_hi * 4 + y_lo), z: 12, core: 2. Of those that a mesh axis runs over, the one named last changes fastest.
Arguments:
- trial: float32 [1, 256, 1024], P(None, None, 'row'), may hold values from -6 to 6
- screened: bfloat16 [18432, 18432], P('row', 'col'), may hold values from -0.15625 to 0.15625
- val_points: bfloat16 [18432, 256], P('row'), may hold values from -0.375 to 0.375
- cond_points: bfloat16 [18432, 1024], P('col', 'row'), may hold values from -0.1875 to 0.1875
- eps_val: float32 [256], replicated, may hold values from -0.6 to -0.1
- eps_cond: float32 [1024], replicated, may hold values from 0.1 to 1
Outputs:
- applied: float32 [1, 256, 1024], P(None, None, 'row')
All inputs are finite; a program needn't handle non-finite values.
Results may differ from a plain program's by a relative error of at most 0.02.
Values may be sent and summed in bfloat16 or wider, within the bound.
No kernel may reach another device: no remote copies, remote signals or barrier semaphores. Data moves between devices by JAX's collectives and lax.ppermute only.
A program may use at most 32 MiB of HBM per device.

v0:
```python
import jax
import jax.numpy as jnp
from jax import lax
from jax.sharding import PartitionSpec as P

APPLY = 2


def sent_to_all(array, axis):
    copies = jnp.broadcast_to(array, (lax.axis_size(axis), *array.shape))
    return lax.all_to_all(copies, axis, split_axis=0, concat_axis=0, tiled=True)


def joined_along(blocks, dim):
    blocks = jnp.moveaxis(blocks, 0, dim)
    dims = blocks.shape
    return blocks.reshape(*dims[:dim], dims[dim] * dims[dim + 1], *dims[dim + 2 :])


def gather_directly(array, axis, dim):
    blocks = sent_to_all(array, axis)
    return joined_along(blocks, dim)


def cut_along(array, dim, devices):
    dims = array.shape
    blocks = array.reshape(*dims[:dim], devices, dims[dim] // devices, *dims[dim + 1 :])
    return jnp.moveaxis(blocks, dim, 0)


def sent_and_summed(array, axis, dim):
    devices = lax.axis_size(axis)
    blocks = lax.all_to_all(cut_along(array, dim, devices), axis, 0, 0, tiled=True)
    return jnp.sum(blocks.astype(jnp.float32), axis=0)


def over_copies(array, axis):
    everything = sent_to_all(array, axis)
    return jnp.sum(everything.astype(jnp.float32), axis=0)


def body(trial, screened, val_points, cond_points, eps_val, eps_cond):
    cond_full = gather_directly(cond_points, "row", 1)
    energy_full = eps_cond[None, :] - eps_val[:, None]
    width = trial.shape[2]
    offset = lax.axis_index("row") * width
    energy_mine = lax.dynamic_slice_in_dim(energy_full, offset, width, 1)
    x_full = gather_directly(trial.astype(jnp.bfloat16), "row", 2).astype(trial.dtype)
    xb_full = x_full.astype(jnp.bfloat16)
    x_mine = trial
    for step in range(APPLY):
        pair = jnp.einsum(
            "mv,bvc->bmc", val_points, xb_full, preferred_element_type=jnp.float32
        ).astype(jnp.bfloat16)
        inner = jnp.einsum("bmc,nc->bmn", pair, cond_full, preferred_element_type=jnp.float32)
        tile = (screened[None] * inner).astype(jnp.bfloat16)
        back = jnp.einsum(
            "bmn,nc->bmc", tile, cond_full, preferred_element_type=jnp.float32
        ).astype(jnp.bfloat16)
        part_low = jnp.einsum(
            "mv,bmc->bvc", val_points, back, preferred_element_type=jnp.float32
        ).astype(jnp.bfloat16)
        partial_terms = lax.optimization_barrier(part_low).astype(jnp.float32)
        kernel_rows = sent_and_summed(partial_terms.astype(jnp.bfloat16), "row", 2)
        kernel_mine = over_copies(kernel_rows.astype(jnp.bfloat16), "col").astype(jnp.float32)
        x_mine = energy_mine[None] * x_mine + kernel_mine
        if step + 1 < APPLY:
            xb_full = gather_directly(x_mine.astype(jnp.bfloat16), "row", 2)
    return x_mine


def solution(mesh):
    in_specs = (P(None, None, "row"), P("row", "col"), P("row", None), P("col", "row"), P(), P())
    out_specs = P(None, None, "row")
    return jax.shard_map(body, mesh=mesh, in_specs=in_specs, out_specs=out_specs, check_vma=False)
```

profile of v0, /device:TPU:8, one launch (start us, length us, event | category | flops | bytes accessed | tf_op | source)
XLA Modules:
  0.0 212.0 jit_solution(15553128472799787133)
XLA Ops:
  0.0 0.0 copy-start
  0.0 0.0 copy-start.2
  0.0 0.8 convert_bitcast_fusion.1
  0.8 0.1 broadcast_in_dim.24
  0.9 27.6 %all_to_all.35 = bf16[32,1,256,32]{2,3,1,0:T(8,128)(2,1)S(1)} all-to-all(bf16[32,1,256,32]{2,3,1,0:T(8,128)(2,1)S(1)} %broadcast_in_dim.24), channel_id=1, replica_groups=mesh['row'=32,'col'=24] {'row'}, dimensions={0} | all-to-all | bytes 1048576 | tf_op jit(solution)/shard_map/all_to_all | solution.py:11
  28.4 0.0 copy-done.2
  28.4 0.2 broadcast_in_dim.25
  28.6 0.0 copy-start.4
  28.6 42.8 %all_to_all.36 = bf16[32,768,32]{1,2,0:T(8,128)(2,1)S(1)} all-to-all(bf16[32,768,32]{1,2,0:T(8,128)(2,1)S(1)} %broadcast_in_dim.25), channel_id=1, replica_groups=mesh['row'=32,'col'=24] {'row'}, dimensions={0} | all-to-all | bytes 3145728 | tf_op jit(solution)/shard_map/all_to_all | solution.py:11
  71.5 0.0 copy-done
  71.5 0.0 copy-done.4
  71.5 2.5 %fusion = bf16[576,768]{1,0:T(8,128)(2,1)} fusion(bf16[576,768]{1,0:T(8,128)(2,1)S(1)} %copy-done.4, bf16[768,1024]{0,1:T(8,128)(2,1)S(1)} %bitcast.86, bf16[256,1024]{0,1:T(8,128)(2,1)S(1)} %bitcast.90, bf16[576,256]{1,0:T(8,128)(2,1)S(1)} %copy-done), kind=kOutput, calls=%fused_computation.2 | convolution fusion | flops 1209876480 | bytes 4161536 | tf_op jit(solution)/shard_map/bmc,nc->bmn/dot_general | solution.py:55
  73.9 2.7 %fusion.4 = bf16[1,256,1024]{1,2,0:T(8,128)(2,1)S(1)} fusion(bf16[576,256]{1,0:T(8,128)(2,1)S(1)} %copy-done, bf16[576,768]{1,0:T(8,128)(2,1)} %fusion, bf16[768,1024]{0,1:T(8,128)(2,1)S(1)} %bitcast.87), kind=kOutput, calls=%fused_computation.12 | convolution fusion | flops 1208811520 | bytes 3276800 | tf_op jit(solution)/shard_map/mv,bmc->bvc/dot_general | solution.py:60
  76.6 0.0 copy-start.1
  76.7 0.0 copy-start.3
  76.7 20.3 %all_to_all.37 = bf16[32,1,256,32]{2,3,1,0:T(8,128)(2,1)S(1)} all-to-all(bf16[32,1,256,32]{2,3,1,0:T(8,128)(2,1)S(1)} %bitcast.92), channel_id=1, replica_groups=mesh['row'=32,'col'=24] {'row'}, dimensions={0} | all-to-all | bytes 1048576 | tf_op jit(solution)/shard_map/all_to_all | solution.py:33
  97.0 0.1 bitcast_reduce_fusion.1
  97.1 0.8 broadcast_in_dim.26
  97.9 13.6 %all-to-all-start.3 = ((bf16[24,1,256,32]{2,3,1,0:T(8,128)(2,1)}), bf16[24,1,256,32]{2,3,1,0:T(8,128)(2,1)S(1)}, u32[]{:S(2)}, u32[]{:S(2)}) async-start(bf16[24,1,256,32]{2,3,1,0:T(8,128)(2,1)} %broadcast_in_dim.26), calls=%async_computation.3 | async-start | bytes 786432 | tf_op jit(solution)/shard_map/all_to_all | solution.py:11
  111.4 0.8 dynamic-slice
  112.2 24.1 %all-to-all-done.3 = bf16[24,1,256,32]{2,3,1,0:T(8,128)(2,1)S(1)} async-done(((bf16[24,1,256,32]{2,3,1,0:T(8,128)(2,1)}), bf16[24,1,256,32]{2,3,1,0:T(8,128)(2,1)S(1)}, u32[]{:S(2)}, u32[]{:S(2)}) %all-to-all-start.3) | async-done | bytes 393248 | tf_op jit(solution)/shard_map/all_to_all | solution.py:11
  136.3 0.1 convert_reduce_fusion.1
  136.3 0.0 copy-done.1
  136.3 0.0 copy-done.3
  136.4 0.1 convert_bitcast_fusion
  136.4 0.1 broadcast_in_dim.27
  136.5 20.2 %all_to_all.38 = bf16[32,1,256,32]{2,3,1,0:T(8,128)(2,1)S(1)} all-to-all(bf16[32,1,256,32]{2,3,1,0:T(8,128)(2,1)S(1)} %broadcast_in_dim.27), channel_id=1, replica_groups=mesh['row'=32,'col'=24] {'row'}, dimensions={0} | all-to-all | bytes 1048576 | tf_op jit(solution)/shard_map/all_to_all | solution.py:11
  156.7 2.5 %fusion.1 = bf16[576,768]{1,0:T(8,128)(2,1)} fusion(bf16[576,768]{1,0:T(8,128)(2,1)S(1)} %copy-done.4, bf16[768,1024]{0,1:T(8,128)(2,1)S(1)} %bitcast.88, bf16[256,1024]{0,1:T(8,128)(2,1)S(1)} %bitcast.93, bf16[576,256]{1,0:T(8,128)(2,1)S(1)} %copy-done), kind=kOutput, calls=%fused_computation.3 | convolution fusion | flops 1209876480 | bytes 4161536 | tf_op jit(solution)/shard_map/bmc,nc->bmn/dot_general | solution.py:55
  159.1 2.7 %fusion.5 = bf16[1,256,1024]{1,2,0:T(8,128)(2,1)S(1)} fusion(bf16[576,256]{1,0:T(8,128)(2,1)S(1)} %copy-done, bf16[576,768]{1,0:T(8,128)(2,1)} %fusion.1, bf16[768,1024]{0,1:T(8,128)(2,1)S(1)} %bitcast.89), kind=kOutput, calls=%fused_computation.13 | convolution fusion | flops 1208811520 | bytes 3276800 | tf_op jit(solution)/shard_map/mv,bmc->bvc/dot_general | solution.py:60
  161.8 20.3 %all_to_all.39 = bf16[32,1,256,32]{2,3,1,0:T(8,128)(2,1)S(1)} all-to-all(bf16[32,1,256,32]{2,3,1,0:T(8,128)(2,1)S(1)} %bitcast.91), channel_id=1, replica_groups=mesh['row'=32,'col'=24] {'row'}, dimensions={0} | all-to-all | bytes 1048576 | tf_op jit(solution)/shard_map/all_to_all | solution.py:33
  182.2 0.1 bitcast_reduce_fusion
  182.3 29.0 %all_to_all.40 = bf16[24,1,256,32]{2,3,1,0:T(8,128)(2,1)S(1)} all-to-all(bf16[24,1,256,32]{2,3,1,0:T(8,128)(2,1)S(1)} %broadcast_in_dim.28), channel_id=1, replica_groups=mesh['row'=32,'col'=24] {'col'}, dimensions={0} | all-to-all | bytes 786432 | tf_op jit(solution)/shard_map/all_to_all | solution.py:11
  211.2 0.1 convert_reduce_fusion
  211.3 0.7 bitcast_add_fusion
  (1 shorter events, 0.0 us)
Async XLA Ops:
  0.0 71.5 %copy-start = (bf16[576,256]{1,0:T(8,128)(2,1)S(1)}, bf16[576,256]{1,0:T(8,128)(2,1)}, u32[]{:S(2)}) copy-start(bf16[576,256]{1,0:T(8,128)(2,1)} %param.8) | copy-start | bytes 884740
  0.0 28.4 %copy-start.2 = (bf16[768,32]{0,1:T(8,128)(2,1)S(1)}, bf16[768,32]{0,1:T(8,128)(2,1)}, u32[]{:S(2)}) copy-start(bf16[768,32]{0,1:T(8,128)(2,1)} %param.9) | copy-start | bytes 147460
  28.6 42.9 %copy-start.4 = (bf16[576,768]{1,0:T(8,128)(2,1)S(1)}, bf16[576,768]{1,0:T(8,128)(2,1)}, u32[]{:S(2)}) copy-start(bf16[576,768]{1,0:T(8,128)(2,1)} %param.7) | copy-start | bytes 2654212
  76.6 59.7 %copy-start.1 = (f32[1,256,32]{1,2,0:T(8,128)S(1)}, f32[1,256,32]{1,2,0:T(8,128)}, u32[]{:S(2)}) copy-start(f32[1,256,32]{1,2,0:T(8,128)} %param.6) | copy-start | bytes 98308
  76.7 59.7 %copy-start.3 = (f32[256]{0:T(256)S(1)}, f32[256]{0:T(256)}, u32[]{:S(2)}) copy-start(f32[256]{0:T(256)} %param.10) | copy-start | bytes 3076
  97.9 38.4 %all-to-all-start.3 = ((bf16[24,1,256,32]{2,3,1,0:T(8,128)(2,1)}), bf16[24,1,256,32]{2,3,1,0:T(8,128)(2,1)S(1)}, u32[]{:S(2)}, u32[]{:S(2)}) async-start(bf16[24,1,256,32]{2,3,1,0:T(8,128)(2,1)} %broadcast_in_dim.26), calls=%async_computation.3 | async-start | bytes 786432 | tf_op jit(solution)/shard_map/all_to_all | solution.py:11
where the time goes:
time: 213 us; the launch traced here: 212 us
  blocking collectives  160 us (75%)
  waiting for transfers between devices  24.1 us (11%)
  starting transfers between devices  13.6 us (6%)
  matrix products  10.3 us (5%)
    all_to_all x4, blocking collectives, sent_to_all(): return lax.all_to_all(copies, axis, split_axis=0, concat_axis=0, tiled=True)  120 us
    all_to_all x2, blocking collectives, sent_and_summed(): lax.all_to_all(cut_along(array, dim, devices), axis, 0, 0, tiled=True)  40.6 us
    all_to_all x1, waiting for transfers between devices, sent_to_all(): return lax.all_to_all(copies, axis, split_axis=0, concat_axis=0, tiled=True)  24.1 us
    all_to_all x1, starting transfers between devices, sent_to_all(): return lax.all_to_all(copies, axis, split_axis=0, concat_axis=0, tiled=True)  13.6 us
    dot_general x2, matrix products, body(): jnp.einsum('mv,bmc->bvc', val_points, back, preferred_element_type=jnp.fl...  5.39 us
    dot_general x2, matrix products, body(): jnp.einsum('bmc,nc->bmn', pair, cond_full, preferred_element_type=jnp.flo...  4.93 us
  transfers between devices with their start and end apart: 1, of which 1 were waited for; matrix products, arithmetic and copies ran while one was open for 0% of the time, Pallas kernels for 0%

commit v1 on v0

v1 whole, which is shorter than its diff:
```python
import jax
import jax.numpy as jnp
from jax import lax
from jax.sharding import Mesh, PartitionSpec as P

APPLY = 2
F32 = jnp.float32
BF16 = jnp.bfloat16

YX = ("ylo", "x")
ROW = ("ylo", "x", "core")
COL = ("yhi", "z")


def copies_from_all(array, axes):
    devices = lax.axis_size(axes)
    copies = jnp.broadcast_to(array, (devices, *array.shape))
    return lax.all_to_all(copies, axes, 0, 0, tiled=True)


def summed_over_copies(array, axes):
    return jnp.sum(copies_from_all(array, axes).astype(F32), axis=0)


def summed_over_pair(array, axis):
    both = lax.all_gather(array, axis, axis=0, tiled=False)
    return both[0].astype(F32) + both[1].astype(F32)


def body(trial, screened, val_points, cond_points, eps_val, eps_cond):
    nv, width = trial.shape[1], trial.shape[2]
    n_cols = cond_points.shape[0]
    peers = lax.axis_size(YX)
    offset = lax.axis_index(ROW) * width
    energy = lax.dynamic_slice_in_dim(eps_cond, offset, width, 0)[:, None] - eps_val[None, :]

    x_mine = trial[0].T
    mine = jnp.concatenate([cond_points.T, x_mine.astype(BF16)], axis=1)
    everything = copies_from_all(mine, YX).reshape(peers * width, n_cols + nv)
    cond_half = everything[:, :n_cols]
    x_half = everything[:, n_cols:]

    for step in range(APPLY):
        mixed_part = jnp.einsum("cv,cn->vn", x_half, cond_half, preferred_element_type=F32)
        mixed = summed_over_pair(mixed_part.astype(BF16), "core").astype(BF16)
        inner = jnp.einsum("mv,vn->mn", val_points, mixed, preferred_element_type=F32)
        tile = (screened * inner).astype(BF16)
        folded_part = jnp.einsum("mv,mn->vn", val_points, tile, preferred_element_type=F32)
        folded = summed_over_pair(folded_part.astype(BF16), "core").astype(BF16)
        terms = jnp.einsum("cn,vn->cv", cond_half, folded, preferred_element_type=F32)
        terms = terms.astype(BF16).reshape(peers, width, nv)
        rows = jnp.sum(lax.all_to_all(terms, YX, 0, 0, tiled=True).astype(F32), axis=0)
        along_z = summed_over_copies(rows.astype(BF16), "z")
        kernel_mine = summed_over_pair(along_z.astype(BF16), "yhi")
        x_mine = energy * x_mine + kernel_mine
        if step + 1 < APPLY:
            x_half = copies_from_all(x_mine.astype(BF16), YX).reshape(peers * width, nv)
    return x_mine.T[None]


def solution(mesh):
    devices = mesh.devices.reshape(4, 4, 2, 2, 12)
    fine = Mesh(devices, ("ylo", "x", "core", "yhi", "z"))
    in_specs = (P(None, None, ROW), P(ROW, COL), P(ROW, None), P(COL, ROW), P(), P())
    out_specs = P(None, None, ROW)
    return jax.shard_map(body, mesh=fine, in_specs=in_specs, out_specs=out_specs, check_vma=False)
```

time: 213 us -> 154 us (0.72)
  the two profiles are of different devices: /device:TPU:8 before, /device:TPU:64 now
where the time goes in v1:
time: 154 us
  blocking collectives  119 us (77%)
  starting transfers between devices  14.8 us (10%)
  waiting for transfers between devices  11.7 us (8%)
  matrix products  3.39 us (2%)
  other arithmetic  2.53 us (2%)
  local copies, waits for them, and re-layouts  1.62 us (1%)
    all_to_all x3, blocking collectives, copies_from_all(): return lax.all_to_all(copies, axes, 0, 0, tiled=True)  64.2 us
    all_to_all x2, blocking collectives, body(): lax.all_to_all(terms, YX, 0, 0, tiled=True).astype(F32)  29.1 us
    all_gather x6, blocking collectives, summed_over_pair(): both = lax.all_gather(array, axis, axis=0, tiled=False)  26.1 us
    all_to_all x1, starting transfers between devices, copies_from_all(): return lax.all_to_all(copies, axes, 0, 0, tiled=True)  14.8 us
    all_to_all x1, waiting for transfers between devices, copies_from_all(): return lax.all_to_all(copies, axes, 0, 0, tiled=True)  11.7 us
  transfers between devices with their start and end apart: 1, of which 1 were waited for; matrix products, arithmetic and copies ran while one was open for 0% of the time, Pallas kernels for 0%

profile of v1, /device:TPU:64, one launch (start us, length us, event | category | flops | bytes accessed | tf_op | source)
XLA Modules:
  0.0 153.6 jit_solution(2216481462259752546)
XLA Ops:
  0.0 0.0 copy-start
  0.0 0.8 bitcast_convert_fusion
  0.8 0.8 pad_maximum_fusion
  1.6 0.1 broadcast_in_dim.17
  1.7 33.9 %all_to_all.30 = bf16[16,32,1024]{2,1,0:T(8,128)(2,1)S(1)} all-to-all(bf16[16,32,1024]{2,1,0:T(8,128)(2,1)S(1)} %broadcast_in_dim.17), channel_id=1, replica_groups=mesh['ylo'=4,'x'=4,'core'=2,'yhi'=2,'z'=12] {'ylo','x'}, dimensions={0} | all-to-all | bytes 2097152 | tf_op jit(solution)/shard_map/all_to_all | solution.py:18
  35.6 0.0 copy-start.3
  35.6 0.4 convolution_convert_fusion.1
  36.0 2.4 %all-gather = bf16[512,768]{1,0:T(8,128)(2,1)S(1)} all-gather(bf16[256,768]{1,0:T(8,128)(2,1)S(1)} %convolution_convert_fusion.1), channel_id=2, replica_groups=mesh['ylo'=4,'x'=4,'core'=2,'yhi'=2,'z'=12] {'core'}, dimensions={0}, use_global_device_ids=true | all-gather | bytes 1179648 | tf_op jit(solution)/shard_map/all_gather | solution.py:26
  38.4 0.0 copy-done
  38.4 0.0 copy-done.3
  38.4 0.9 fusion.7
  39.3 2.4 %all-gather.1 = bf16[512,768]{0,1:T(8,128)(2,1)S(1)} all-gather(bf16[256,768]{0,1:T(8,128)(2,1)S(1)} %fusion.7), channel_id=3, replica_groups=mesh['ylo'=4,'x'=4,'core'=2,'yhi'=2,'z'=12] {'core'}, dimensions={0}, use_global_device_ids=true | all-gather | bytes 1179648 | tf_op jit(solution)/shard_map/all_gather | solution.py:26
  41.7 0.4 convolution_convert_fusion.3
  42.1 0.0 copy-start.1
  42.1 0.0 copy-start.2
  42.1 15.3 %all_to_all.31 = bf16[16,32,256]{2,1,0:T(8,128)(2,1)S(1)} all-to-all(bf16[16,32,256]{2,1,0:T(8,128)(2,1)S(1)} %bitcast.48), channel_id=1, replica_groups=mesh['ylo'=4,'x'=4,'core'=2,'yhi'=2,'z'=12] {'ylo','x'}, dimensions={0} | all-to-all | bytes 524288 | tf_op jit(solution)/shard_map/all_to_all | solution.py:52
  57.4 0.7 broadcast_in_dim.18
  58.1 14.8 %all-to-all-start.2 = ((bf16[12,32,256]{2,1,0:T(8,128)(2,1)}), bf16[12,32,256]{2,1,0:T(8,128)(2,1)S(1)}, u32[]{:S(2)}, u32[]{:S(2)}) async-start(bf16[12,32,256]{2,1,0:T(8,128)(2,1)} %broadcast_in_dim.18), calls=%async_computation.2 | async-start | bytes 393216 | tf_op jit(solution)/shard_map/all_to_all | solution.py:18
  72.9 0.8 dynamic_slice.3
  73.6 11.7 %all-to-all-done.2 = bf16[12,32,256]{2,1,0:T(8,128)(2,1)S(1)} async-done(((bf16[12,32,256]{2,1,0:T(8,128)(2,1)}), bf16[12,32,256]{2,1,0:T(8,128)(2,1)S(1)}, u32[]{:S(2)}, u32[]{:S(2)}) %all-to-all-start.2) | async-done | bytes 196640 | tf_op jit(solution)/shard_map/all_to_all | solution.py:18
  85.4 8.3 %all-gather.2 = bf16[64,256]{1,0:T(8,128)(2,1)S(1)} all-gather(bf16[32,256]{1,0:T(8,128)(2,1)S(1)} %reduce_sum.49), channel_id=4, replica_groups=mesh['ylo'=4,'x'=4,'core'=2,'yhi'=2,'z'=12] {'yhi'}, dimensions={0}, use_global_device_ids=true | all-gather | bytes 49152 | tf_op jit(solution)/shard_map/all_gather | solution.py:26
  93.7 0.0 copy-done.1
  93.7 0.0 copy-done.2
  93.7 0.1 fusion.28
  93.8 14.3 %all_to_all.32 = bf16[16,32,256]{2,1,0:T(8,128)(2,1)S(1)} all-to-all(bf16[16,32,256]{2,1,0:T(8,128)(2,1)S(1)} %broadcast_in_dim.19), channel_id=1, replica_groups=mesh['ylo'=4,'x'=4,'core'=2,'yhi'=2,'z'=12] {'ylo','x'}, dimensions={0} | all-to-all | bytes 524288 | tf_op jit(solution)/shard_map/all_to_all | solution.py:18
  108.1 0.4 convolution_convert_fusion
  108.5 2.4 %all-gather.3 = bf16[512,768]{1,0:T(8,128)(2,1)S(1)} all-gather(bf16[256,768]{1,0:T(8,128)(2,1)S(1)} %convolution_convert_fusion), channel_id=5, replica_groups=mesh['ylo'=4,'x'=4,'core'=2,'yhi'=2,'z'=12] {'core'}, dimensions={0}, use_global_device_ids=true | all-gather | bytes 1179648 | tf_op jit(solution)/shard_map/all_gather | solution.py:26
  110.9 0.9 fusion.6
  111.8 2.4 %all-gather.4 = bf16[512,768]{0,1:T(8,128)(2,1)S(1)} all-gather(bf16[256,768]{0,1:T(8,128)(2,1)S(1)} %fusion.6), channel_id=6, replica_groups=mesh['ylo'=4,'x'=4,'core'=2,'yhi'=2,'z'=12] {'core'}, dimensions={0}, use_global_device_ids=true | all-gather | bytes 1179648 | tf_op jit(solution)/shard_map/all_gather | solution.py:26
  114.2 0.4 convolution_convert_fusion.2
  114.6 13.9 %all_to_all.33 = bf16[16,32,256]{2,1,0:T(8,128)(2,1)S(1)} all-to-all(bf16[16,32,256]{2,1,0:T(8,128)(2,1)S(1)} %bitcast.47), channel_id=1, replica_groups=mesh['ylo'=4,'x'=4,'core'=2,'yhi'=2,'z'=12] {'ylo','x'}, dimensions={0} | all-to-all | bytes 524288 | tf_op jit(solution)/shard_map/all_to_all | solution.py:52
  128.5 16.0 %all_to_all.34 = bf16[12,32,256]{2,1,0:T(8,128)(2,1)S(1)} all-to-all(bf16[12,32,256]{2,1,0:T(8,128)(2,1)S(1)} %broadcast_in_dim.20), channel_id=1, replica_groups=mesh['ylo'=4,'x'=4,'core'=2,'yhi'=2,'z'=12] {'z'}, dimensions={0} | all-to-all | bytes 393216 | tf_op jit(solution)/shard_map/all_to_all | solution.py:18
  144.6 8.3 %all-gather.5 = bf16[64,256]{1,0:T(8,128)(2,1)S(1)} all-gather(bf16[32,256]{1,0:T(8,128)(2,1)S(1)} %reduce_sum.51), channel_id=7, replica_groups=mesh['ylo'=4,'x'=4,'core'=2,'yhi'=2,'z'=12] {'yhi'}, dimensions={0}, use_global_device_ids=true | all-gather | bytes 49152 | tf_op jit(solution)/shard_map/all_gather | solution.py:26
  152.9 0.7 fusion.27
  (6 shorter events, 0.2 us)
Async XLA Ops:
  0.0 38.4 %copy-start = (bf16[576,256]{1,0:T(8,128)(2,1)S(1)}, bf16[576,256]{1,0:T(8,128)(2,1)}, u32[]{:S(2)}) copy-start(bf16[576,256]{1,0:T(8,128)(2,1)} %param.8) | copy-start | bytes 884740
  35.6 2.8 %copy-start.3 = (bf16[576,768]{1,0:T(8,128)(2,1)S(1)}, bf16[576,768]{1,0:T(8,128)(2,1)}, u32[]{:S(2)}) copy-start(bf16[576,768]{1,0:T(8,128)(2,1)} %param.7) | copy-start | bytes 2654212
  42.1 51.7 %copy-start.1 = (f32[1,256,32]{1,2,0:T(8,128)S(1)}, f32[1,256,32]{1,2,0:T(8,128)}, u32[]{:S(2)}) copy-start(f32[1,256,32]{1,2,0:T(8,128)} %param.6) | copy-start | bytes 98308
  42.1 51.7 %copy-start.2 = (f32[256]{0:T(256)S(1)}, f32[256]{0:T(256)}, u32[]{:S(2)}) copy-start(f32[256]{0:T(256)} %param.10) | copy-start | bytes 3076
  58.1 27.3 %all-to-all-start.2 = ((bf16[12,32,256]{2,1,0:T(8,128)(2,1)}), bf16[12,32,256]{2,1,0:T(8,128)(2,1)S(1)}, u32[]{:S(2)}, u32[]{:S(2)}) async-start(bf16[12,32,256]{2,1,0:T(8,128)(2,1)} %broadcast_in_dim.18), calls=%async_computation.2 | async-start | bytes 393216 | tf_op jit(solution)/shard_map/all_to_all | solution.py:18

commit v2 on v1

v2 whole, which is shorter than its diff:
```python
import jax
import jax.numpy as jnp
from jax import lax
from jax.sharding import Mesh, PartitionSpec as P

APPLY = 2
F32 = jnp.float32
BF16 = jnp.bfloat16

ROW = ("y2", "y1", "x", "core")
COL = ("yhi", "z")
NEAR = ("y1", "x")
PLANE = ("y1", "x", "y2")
WIDE = ("y1", "x", "y2", "yhi")


def copies_from_all(array, axes):
    devices = lax.axis_size(axes)
    copies = jnp.broadcast_to(array, (devices, *array.shape))
    return lax.all_to_all(copies, axes, 0, 0, tiled=True)


def summed_over_copies(array, axes):
    return jnp.sum(copies_from_all(array, axes).astype(F32), axis=0)


def summed_over_pair(array, axis):
    both = lax.all_gather(array, axis, axis=0, tiled=False)
    return both[0].astype(F32) + both[1].astype(F32)


def sent_and_summed(blocks, axes):
    return jnp.sum(lax.all_to_all(blocks, axes, 0, 0, tiled=True).astype(F32), axis=0)


def rows_from(array, start, rows):
    return lax.dynamic_slice(array, (start, jnp.uint32(0)), (rows, array.shape[1]))


def body(trial, screened, val_points, cond_points, eps_val, eps_cond):
    nv, width = trial.shape[1], trial.shape[2]
    n_cols = cond_points.shape[0]
    blocks = lax.axis_size(PLANE)
    half = width // 2
    offset = lax.axis_index(ROW) * width
    energy = lax.dynamic_slice_in_dim(eps_cond, offset, width, 0)[:, None] - eps_val[None, :]

    x_mine = trial[0].T
    mine = jnp.concatenate([cond_points.T, x_mine.astype(BF16)], axis=1)
    piece = lax.convert_element_type(lax.axis_index("yhi") * half, jnp.uint32)
    own = lax.convert_element_type(lax.axis_index(PLANE) * width, jnp.uint32)
    mine, energy, piece, own = lax.optimization_barrier((mine, energy, piece, own))
    two = lax.all_gather(mine, "y2", axis=0, tiled=False)
    everything = copies_from_all(two, NEAR).reshape(blocks * width, n_cols + nv)
    cond_half = everything[:, :n_cols]
    x_half = everything[:, n_cols:]

    def terms_of(x_half):
        mixed_part = jnp.einsum("cv,cn->vn", x_half, cond_half, preferred_element_type=F32)
        mixed = summed_over_pair(mixed_part.astype(BF16), "core").astype(BF16)
        inner = jnp.einsum("mv,vn->mn", val_points, mixed, preferred_element_type=F32)
        tile = (screened * inner).astype(BF16)
        folded_part = jnp.einsum("mv,mn->vn", val_points, tile, preferred_element_type=F32)
        folded = summed_over_pair(folded_part.astype(BF16), "core").astype(BF16)
        terms = jnp.einsum("cn,vn->cv", cond_half, folded, preferred_element_type=F32)
        return terms.astype(BF16)

    x_piece = rows_from(x_mine, piece, half)
    energy_piece = rows_from(energy, piece, half)
    for _ in range(APPLY - 1):
        terms = terms_of(x_half).reshape(2 * blocks, half, nv)
        rows = sent_and_summed(terms, WIDE)
        x_piece = energy_piece * x_piece + summed_over_copies(rows.astype(BF16), "z")
        x_half = copies_from_all(x_piece.astype(BF16), WIDE).reshape(blocks * width, nv)

    terms = terms_of(x_half).reshape(blocks, 1, width, nv)
    twice = jnp.broadcast_to(terms, (blocks, 2, width, nv)).reshape(2 * blocks, width, nv)
    rows = sent_and_summed(twice, WIDE)
    x_mine = rows_from(x_half, own, width)
    x_mine = energy * x_mine.astype(F32) + summed_over_copies(rows.astype(BF16), "z")
    return x_mine.T[None]


def solution(mesh):
    devices = mesh.devices.reshape(2, 2, 4, 2, 2, 12)
    fine = Mesh(devices, ("y2", "y1", "x", "core", "yhi", "z"))
    in_specs = (P(None, None, ROW), P(ROW, COL), P(ROW, None), P(COL, ROW), P(), P())
    out_specs = P(None, None, ROW)
    return jax.shard_map(body, mesh=fine, in_specs=in_specs, out_specs=out_specs, check_vma=False)
```

time: 154 us -> 146 us (0.948)
  the two profiles are of different devices: /device:TPU:64 before, /device:TPU:8 now
where the time goes in v2:
time: 146 us; the launch traced here: 145 us
  blocking collectives  136 us (93%)
  matrix products  4.53 us (3%)
  other arithmetic  3.2 us (2%)
    all_to_all x4, blocking collectives, copies_from_all(): return lax.all_to_all(copies, axes, 0, 0, tiled=True)  79.5 us
    all_to_all x2, blocking collectives, sent_and_summed(): lax.all_to_all(blocks, axes, 0, 0, tiled=True).astype(F32)  41.6 us
    all_gather x4, blocking collectives, summed_over_pair(): both = lax.all_gather(array, axis, axis=0, tiled=False)  9.48 us
    all_gather x1, blocking collectives, body(): two = lax.all_gather(mine, 'y2', axis=0, tiled=False)  5.82 us
    dot_general x2, matrix products, terms_of(): jnp.einsum('mv,mn->vn', val_points, tile, preferred_element_type=F32)  2.95 us

profile of v2, /device:TPU:8, one launch (start us, length us, event | category | flops | bytes accessed | tf_op | source)
XLA Modules:
  0.0 145.2 jit_solution(9976068646877321092)
XLA Ops:
  0.0 0.0 copy-start
  0.0 0.8 convert_bitcast_fusion
  0.8 0.8 dynamic_slice.12
  1.6 0.7 broadcast_subtract_fusion
  2.3 0.8 pad_maximum_fusion
  3.1 5.8 %all-gather = bf16[64,1024]{1,0:T(8,128)(2,1)S(1)} all-gather(bf16[32,1024]{1,0:T(8,128)(2,1)S(1)} %pad_maximum_fusion), channel_id=2, replica_groups=mesh['y2'=2,'y1'=2,'x'=4,'core'=2,'yhi'=2,'z'=12] {'y2'}, dimensions={0}, use_global_device_ids=true | all-gather | bytes 196608 | tf_op jit(solution)/shard_map/all_gather | solution.py:53
  8.9 0.1 broadcast_in_dim.24
  9.1 22.0 %all_to_all.30 = bf16[8,2,32,1024]{3,2,1,0:T(8,128)(2,1)S(1)} all-to-all(bf16[8,2,32,1024]{3,2,1,0:T(8,128)(2,1)S(1)} %broadcast_in_dim.24), channel_id=1, replica_groups=mesh['y2'=2,'y1'=2,'x'=4,'core'=2,'yhi'=2,'z'=12] {'y1','x'}, dimensions={0} | all-to-all | bytes 2097152 | tf_op jit(solution)/shard_map/all_to_all | solution.py:20
  31.1 0.0 copy-start.2
  31.1 0.4 convolution_convert_fusion.1
  31.5 2.4 %all-gather.1 = bf16[512,768]{1,0:T(8,128)(2,1)S(1)} all-gather(bf16[256,768]{1,0:T(8,128)(2,1)S(1)} %convolution_convert_fusion.1), channel_id=3, replica_groups=mesh['y2'=2,'y1'=2,'x'=4,'core'=2,'yhi'=2,'z'=12] {'core'}, dimensions={0}, use_global_device_ids=true | all-gather | bytes 1179648 | tf_op jit(solution)/shard_map/all_gather | solution.py:28
  33.8 0.0 copy-done
  33.8 0.0 copy-done.2
  33.8 0.9 fusion.7
  34.7 2.4 %all-gather.2 = bf16[512,768]{0,1:T(8,128)(2,1)S(1)} all-gather(bf16[256,768]{0,1:T(8,128)(2,1)S(1)} %fusion.7), channel_id=4, replica_groups=mesh['y2'=2,'y1'=2,'x'=4,'core'=2,'yhi'=2,'z'=12] {'core'}, dimensions={0}, use_global_device_ids=true | all-gather | bytes 1179648 | tf_op jit(solution)/shard_map/all_gather | solution.py:28
  37.1 0.4 convolution_convert_fusion.3
  37.5 0.0 copy-start.1
  37.5 19.3 %all_to_all.31 = bf16[32,16,256]{2,1,0:T(8,128)(2,1)S(1)} all-to-all(bf16[32,16,256]{2,1,0:T(8,128)(2,1)S(1)} %bitcast.57), channel_id=1, replica_groups=mesh['y2'=2,'y1'=2,'x'=4,'core'=2,'yhi'=2,'z'=12] {'y1','x','y2','yhi'}, dimensions={0} | all-to-all | bytes 524288 | tf_op jit(solution)/shard_map/all_to_all | solution.py:33
  56.8 0.1 reduce_sum.42
  56.8 26.6 %all_to_all.32 = bf16[12,16,256]{2,1,0:T(8,128)(2,1)S(1)} all-to-all(bf16[12,16,256]{2,1,0:T(8,128)(2,1)S(1)} %broadcast_in_dim.25), channel_id=1, replica_groups=mesh['y2'=2,'y1'=2,'x'=4,'core'=2,'yhi'=2,'z'=12] {'z'}, dimensions={0} | all-to-all | bytes 196608 | tf_op jit(solution)/shard_map/all_to_all | solution.py:20
  83.4 0.0 copy-done.1
  83.5 14.8 %all_to_all.33 = bf16[32,16,256]{2,1,0:T(8,128)(2,1)S(1)} all-to-all(bf16[32,16,256]{2,1,0:T(8,128)(2,1)S(1)} %broadcast_in_dim.26), channel_id=1, replica_groups=mesh['y2'=2,'y1'=2,'x'=4,'core'=2,'yhi'=2,'z'=12] {'y1','x','y2','yhi'}, dimensions={0} | all-to-all | bytes 524288 | tf_op jit(solution)/shard_map/all_to_all | solution.py:20
  98.3 0.4 convolution_convert_fusion
  98.7 2.4 %all-gather.3 = bf16[512,768]{1,0:T(8,128)(2,1)S(1)} all-gather(bf16[256,768]{1,0:T(8,128)(2,1)S(1)} %convolution_convert_fusion), channel_id=5, replica_groups=mesh['y2'=2,'y1'=2,'x'=4,'core'=2,'yhi'=2,'z'=12] {'core'}, dimensions={0}, use_global_device_ids=true | all-gather | bytes 1179648 | tf_op jit(solution)/shard_map/all_gather | solution.py:28
  101.1 2.1 %fusion.6 = bf16[256,768]{0,1:T(8,128)(2,1)S(1)} fusion(bf16[576,256]{1,0:T(8,128)(2,1)S(1)} %copy-done, bf16[576,768]{1,0:T(8,128)(2,1)} %param.7, bf16[512,768]{1,0:T(8,128)(2,1)S(1)} %all-gather.3), kind=kOutput, calls=%fused_computation.10 | convolution fusion | flops 455294976 | bytes 2654208 | tf_op jit(solution)/shard_map/mv,mn->vn/dot_general | solution.py:63
  103.2 2.4 %all-gather.4 = bf16[512,768]{0,1:T(8,128)(2,1)S(1)} all-gather(bf16[256,768]{0,1:T(8,128)(2,1)S(1)} %fusion.6), channel_id=6, replica_groups=mesh['y2'=2,'y1'=2,'x'=4,'core'=2,'yhi'=2,'z'=12] {'core'}, dimensions={0}, use_global_device_ids=true | all-gather | bytes 1179648 | tf_op jit(solution)/shard_map/all_gather | solution.py:28
  105.5 0.4 convolution_convert_fusion.2
  105.9 0.1 broadcast_in_dim.28
  106.0 22.3 %all_to_all.34 = bf16[32,32,256]{2,1,0:T(8,128)(2,1)S(1)} all-to-all(bf16[32,32,256]{2,1,0:T(8,128)(2,1)S(1)} %bitcast.48), channel_id=1, replica_groups=mesh['y2'=2,'y1'=2,'x'=4,'core'=2,'yhi'=2,'z'=12] {'y1','x','y2','yhi'}, dimensions={0} | all-to-all | bytes 1048576 | tf_op jit(solution)/shard_map/all_to_all | solution.py:33
  128.3 0.1 reduce_sum.44
  128.4 16.1 %all_to_all.35 = bf16[12,32,256]{2,1,0:T(8,128)(2,1)S(1)} all-to-all(bf16[12,32,256]{2,1,0:T(8,128)(2,1)S(1)} %broadcast_in_dim.29), channel_id=1, replica_groups=mesh['y2'=2,'y1'=2,'x'=4,'core'=2,'yhi'=2,'z'=12] {'z'}, dimensions={0} | all-to-all | bytes 393216 | tf_op jit(solution)/shard_map/all_to_all | solution.py:20
  144.6 0.6 add_bitcast_fusion
  (6 shorter events, 0.1 us)
Async XLA Ops:
  0.0 33.8 %copy-start = (bf16[576,256]{1,0:T(8,128)(2,1)S(1)}, bf16[576,256]{1,0:T(8,128)(2,1)}, u32[]{:S(2)}) copy-start(bf16[576,256]{1,0:T(8,128)(2,1)} %param.8) | copy-start | bytes 884740
  31.1 2.8 %copy-start.2 = (bf16[576,768]{1,0:T(8,128)(2,1)S(1)}, bf16[576,768]{1,0:T(8,128)(2,1)}, u32[]{:S(2)}) copy-start(bf16[576,768]{1,0:T(8,128)(2,1)} %param.7) | copy-start | bytes 2654212
  37.5 45.9 %copy-start.1 = (f32[1,256,32]{1,2,0:T(8,128)S(1)}, f32[1,256,32]{1,2,0:T(8,128)}, u32[]{:S(2)}) copy-start(f32[1,256,32]{1,2,0:T(8,128)} %param.6) | copy-start | bytes 98308

commit v3 on v2

--- a/solution.py
+++ b/solution.py
@@ -1,6 +1,8 @@
 import jax
 import jax.numpy as jnp
 from jax import lax
+from jax.experimental import pallas as pl
+from jax.experimental.pallas import tpu as pltpu
 from jax.sharding import Mesh, PartitionSpec as P
 
 APPLY = 2
@@ -13,6 +15,62 @@
 PLANE = ("y1", "x", "y2")
 WIDE = ("y1", "x", "y2", "yhi")
 
+VMEM = pl.BlockSpec(memory_space=pltpu.VMEM)
+
+
+def start_kernel(offset_ref, trial_ref, cond_ref, val_ref, levels_ref, mine_ref, energy_ref):
+    width, n_cols = cond_ref.shape
+    lanes = levels_ref.shape[1]
+    mine_ref[:, :n_cols] = cond_ref[...]
+    mine_ref[:, n_cols:] = trial_ref[...].astype(BF16)
+    offset = offset_ref[0]
+    group = levels_ref[pl.ds(offset // lanes, 1), :]
+    lane = lax.broadcasted_iota(jnp.int32, (width, lanes), 1)
+    row = lax.broadcasted_iota(jnp.int32, (width, lanes), 0)
+    picked = jnp.where(lane == row + offset % lanes, group, 0.0)
+    energy_ref[...] = jnp.sum(picked, axis=1, keepdims=True) - val_ref[...]
+
+
+def start(offset, trial, cond, eps_val, eps_cond):
+    width, n_cols = cond.shape
+    nv = trial.shape[1]
+    lanes = 128
+    return pl.pallas_call(
+        start_kernel,
+        out_shape=(
+            jax.ShapeDtypeStruct((width, n_cols + nv), BF16),
+            jax.ShapeDtypeStruct((width, nv), F32),
+        ),
+        in_specs=[pl.BlockSpec(memory_space=pltpu.SMEM), VMEM, VMEM, VMEM, VMEM],
+        out_specs=(VMEM, VMEM),
+        compiler_params=pltpu.CompilerParams(vmem_limit_bytes=1 << 20),
+        name="start",
+    )(offset, trial, cond, eps_val.reshape(1, nv), eps_cond.reshape(-1, lanes))
+
+
+def tile_kernel(both_ref, val_ref, screened_ref, out_ref, tile):
+    nv = out_ref.shape[0]
+    mixed = (both_ref[:nv, :].astype(F32) + both_ref[nv:, :].astype(F32)).astype(BF16)
+    inner = jnp.dot(val_ref[...], mixed, preferred_element_type=F32)
+    tile[...] = (screened_ref[...].astype(F32) * inner).astype(BF16)
+    folded = lax.dot_general(val_ref[...], tile[...], (((0,), (0,)), ((), ())), preferred_element_type=F32)
+    out_ref[...] = folded.astype(BF16)
+
+
+def folded_tile(both, val_points, screened):
+    m, nv = val_points.shape
+    n = screened.shape[1]
+    return pl.pallas_call(
+        tile_kernel,
+        out_shape=jax.ShapeDtypeStruct((nv, n), BF16),
+        in_specs=[VMEM, VMEM, VMEM],
+        out_specs=VMEM,
+        scratch_shapes=[pltpu.VMEM((m, n), BF16)],
+        compiler_params=pltpu.CompilerParams(vmem_limit_bytes=16 << 20),
+        cost_estimate=pl.CostEstimate(flops=4 * m * n * nv, bytes_accessed=2 * m * n, transcendentals=0),
+        name="tile",
+    )(both.reshape(2 * nv, n), val_points, screened)
+
 
 def copies_from_all(array, axes):
     devices = lax.axis_size(axes)
@@ -22,11 +80,6 @@
 
 def summed_over_copies(array, axes):
     return jnp.sum(copies_from_all(array, axes).astype(F32), axis=0)
-
-
-def summed_over_pair(array, axis):
-    both = lax.all_gather(array, axis, axis=0, tiled=False)
-    return both[0].astype(F32) + both[1].astype(F32)
 
 
 def sent_and_summed(blocks, axes):
@@ -42,11 +95,10 @@
     n_cols = cond_points.shape[0]
     blocks = lax.axis_size(PLANE)
     half = width // 2
-    offset = lax.axis_index(ROW) * width
-    energy = lax.dynamic_slice_in_dim(eps_cond, offset, width, 0)[:, None] - eps_val[None, :]
 
     x_mine = trial[0].T
-    mine = jnp.concatenate([cond_points.T, x_mine.astype(BF16)], axis=1)
+    offset = (lax.axis_index(ROW) * width).reshape(1)
+    mine, energy = start(offset, x_mine, cond_points.T, eps_val, eps_cond)
     piece = lax.convert_element_type(lax.axis_index("yhi") * half, jnp.uint32)
     own = lax.convert_element_type(lax.axis_index(PLANE) * width, jnp.uint32)
     mine, energy, piece, own = lax.optimization_barrier((mine, energy, piece, own))
@@ -57,11 +109,10 @@
 
     def terms_of(x_half):
         mixed_part = jnp.einsum("cv,cn->vn", x_half, cond_half, preferred_element_type=F32)
-        mixed = summed_over_pair(mixed_part.astype(BF16), "core").astype(BF16)
-        inner = jnp.einsum("mv,vn->mn", val_points, mixed, preferred_element_type=F32)
-        tile = (screened * inner).astype(BF16)
-        folded_part = jnp.einsum("mv,mn->vn", val_points, tile, preferred_element_type=F32)
-        folded = summed_over_pair(folded_part.astype(BF16), "core").astype(BF16)
+        both = lax.all_gather(mixed_part.astype(BF16), "core", axis=0, tiled=False)
+        folded_part = folded_tile(both, val_points, screened)
+        both = lax.all_gather(folded_part, "core", axis=0, tiled=False)
+        folded = (both[0].astype(F32) + both[1].astype(F32)).astype(BF16)
         terms = jnp.einsum("cn,vn->cv", cond_half, folded, preferred_element_type=F32)
         return terms.astype(BF16)
 

time: 146 us -> 143 us (0.979)
  matrix products: 4.53 us -> 1.6 us
  other arithmetic: 3.2 us -> 0.84 us
  Pallas kernels: 0 us -> 1.54 us
    dot_general x2 -> x0, matrix products: 2.95 us -> none  [terms_of(): jnp.einsum('mv,mn->vn', val_points, tile, preferred_element_type=F32)]
    unnamed x6 -> x12, local copies, waits for them, and re-layouts: 0.01 us -> 1.57 us
    pallas_call x0 -> x3, Pallas kernels: none -> 1.54 us  [the longest x2 1.46 us: folded_tile(): pl.pallas_call(tile_kernel, out_shape=jax.ShapeDtypeStruct((nv, n), BF16)...]
where the time goes in v3:
time: 143 us; the launch traced here: 142 us
  blocking collectives  137 us (96%)
  local copies, waits for them, and re-layouts  1.78 us (1%)
  matrix products  1.6 us (1%)
  Pallas kernels  1.54 us (1%)
    all_to_all x4, blocking collectives, copies_from_all(): return lax.all_to_all(copies, axes, 0, 0, tiled=True)  79.5 us
    all_to_all x2, blocking collectives, sent_and_summed(): lax.all_to_all(blocks, axes, 0, 0, tiled=True).astype(F32)  41.6 us
    all_gather x1, blocking collectives, body(): two = lax.all_gather(mine, 'y2', axis=0, tiled=False)  5.82 us
    all_gather x2, blocking collectives, terms_of(): both = lax.all_gather(mixed_part.astype(BF16), 'core', axis=0, tiled=False)  4.87 us
    all_gather x2, blocking collectives, terms_of(): both = lax.all_gather(folded_part, 'core', axis=0, tiled=False)  4.74 us

profile of v3, /device:TPU:8, one launch (start us, length us, event | category | flops | bytes accessed | tf_op | source)
XLA Modules:
  0.0 142.4 jit_solution(2747992469341469968)
XLA Ops:
  0.0 0.0 copy-start.2
  0.0 0.0 copy-start.4
  0.0 0.0 copy-start.5
  0.0 0.7 copy-done.2
  0.8 0.0 copy-done.4
  0.8 0.0 copy-done.5
  0.8 0.0 copy-start.3
  0.8 0.8 copy-done.3
  1.6 0.1 start.1
  1.7 5.8 %all-gather = bf16[64,1024]{1,0:T(8,128)(2,1)S(1)} all-gather(bf16[32,1024]{1,0:T(8,128)(2,1)S(1)} %get-tuple-element.15), channel_id=2, replica_groups=mesh['y2'=2,'y1'=2,'x'=4,'core'=2,'yhi'=2,'z'=12] {'y2'}, dimensions={0}, use_global_device_ids=true | all-gather | bytes 196608 | tf_op jit(solution)/shard_map/all_gather | solution.py:105
  7.5 0.1 broadcast_in_dim.22
  7.6 22.0 %all_to_all.30 = bf16[8,2,32,1024]{3,2,1,0:T(8,128)(2,1)S(1)} all-to-all(bf16[8,2,32,1024]{3,2,1,0:T(8,128)(2,1)S(1)} %broadcast_in_dim.22), channel_id=1, replica_groups=mesh['y2'=2,'y1'=2,'x'=4,'core'=2,'yhi'=2,'z'=12] {'y1','x'}, dimensions={0} | all-to-all | bytes 2097152 | tf_op jit(solution)/shard_map/all_to_all | solution.py:78
  29.6 0.4 convolution_convert_fusion.1
  30.0 0.0 copy-start
  30.0 0.0 copy-start.1
  30.0 2.5 %all-gather.1.both_ref = bf16[512,768]{1,0:T(8,128)(2,1)S(1)} all-gather(bf16[256,768]{1,0:T(8,128)(2,1)S(1)} %convolution_convert_fusion.1), channel_id=3, replica_groups=mesh['y2'=2,'y1'=2,'x'=4,'core'=2,'yhi'=2,'z'=12] {'core'}, dimensions={0}, use_global_device_ids=true | all-gather | bytes 1179648 | tf_op jit(solution)/shard_map/all_gather | solution.py:112
  32.5 0.0 copy-done
  32.5 0.0 copy-done.1
  32.5 0.7 tile.2
  33.3 2.4 %all-gather.2 = bf16[512,768]{1,0:T(8,128)(2,1)S(1)} all-gather(bf16[256,768]{1,0:T(8,128)(2,1)S(1)} %tile.2), channel_id=4, replica_groups=mesh['y2'=2,'y1'=2,'x'=4,'core'=2,'yhi'=2,'z'=12] {'core'}, dimensions={0}, use_global_device_ids=true | all-gather | bytes 1179648 | tf_op jit(solution)/shard_map/all_gather | solution.py:114
  35.6 0.4 convolution_convert_fusion.3
  36.0 19.3 %all_to_all.31 = bf16[32,16,256]{2,1,0:T(8,128)(2,1)S(1)} all-to-all(bf16[32,16,256]{2,1,0:T(8,128)(2,1)S(1)} %bitcast.39), channel_id=1, replica_groups=mesh['y2'=2,'y1'=2,'x'=4,'core'=2,'yhi'=2,'z'=12] {'y1','x','y2','yhi'}, dimensions={0} | all-to-all | bytes 524288 | tf_op jit(solution)/shard_map/all_to_all | solution.py:86
  55.3 0.1 reduce_sum.42
  55.4 26.6 %all_to_all.32 = bf16[12,16,256]{2,1,0:T(8,128)(2,1)S(1)} all-to-all(bf16[12,16,256]{2,1,0:T(8,128)(2,1)S(1)} %broadcast_in_dim.23), channel_id=1, replica_groups=mesh['y2'=2,'y1'=2,'x'=4,'core'=2,'yhi'=2,'z'=12] {'z'}, dimensions={0} | all-to-all | bytes 196608 | tf_op jit(solution)/shard_map/all_to_all | solution.py:78
  82.0 14.8 %all_to_all.33 = bf16[32,16,256]{2,1,0:T(8,128)(2,1)S(1)} all-to-all(bf16[32,16,256]{2,1,0:T(8,128)(2,1)S(1)} %broadcast_in_dim.24), channel_id=1, replica_groups=mesh['y2'=2,'y1'=2,'x'=4,'core'=2,'yhi'=2,'z'=12] {'y1','x','y2','yhi'}, dimensions={0} | all-to-all | bytes 524288 | tf_op jit(solution)/shard_map/all_to_all | solution.py:78
  96.9 0.4 convolution_convert_fusion
  97.3 2.4 %all-gather.3.both_ref = bf16[512,768]{1,0:T(8,128)(2,1)S(1)} all-gather(bf16[256,768]{1,0:T(8,128)(2,1)S(1)} %convolution_convert_fusion), channel_id=5, replica_groups=mesh['y2'=2,'y1'=2,'x'=4,'core'=2,'yhi'=2,'z'=12] {'core'}, dimensions={0}, use_global_device_ids=true | all-gather | bytes 1179648 | tf_op jit(solution)/shard_map/all_gather | solution.py:112
  99.6 0.7 tile.3
  100.4 2.4 %all-gather.4 = bf16[512,768]{1,0:T(8,128)(2,1)S(1)} all-gather(bf16[256,768]{1,0:T(8,128)(2,1)S(1)} %tile.3), channel_id=6, replica_groups=mesh['y2'=2,'y1'=2,'x'=4,'core'=2,'yhi'=2,'z'=12] {'core'}, dimensions={0}, use_global_device_ids=true | all-gather | bytes 1179648 | tf_op jit(solution)/shard_map/all_gather | solution.py:114
  102.7 0.4 convolution_convert_fusion.2
  103.1 0.1 broadcast_in_dim.26
  103.2 22.3 %all_to_all.34 = bf16[32,32,256]{2,1,0:T(8,128)(2,1)S(1)} all-to-all(bf16[32,32,256]{2,1,0:T(8,128)(2,1)S(1)} %bitcast.30), channel_id=1, replica_groups=mesh['y2'=2,'y1'=2,'x'=4,'core'=2,'yhi'=2,'z'=12] {'y1','x','y2','yhi'}, dimensions={0} | all-to-all | bytes 1048576 | tf_op jit(solution)/shard_map/all_to_all | solution.py:86
  125.5 0.1 reduce_sum.44
  125.6 16.1 %all_to_all.35 = bf16[12,32,256]{2,1,0:T(8,128)(2,1)S(1)} all-to-all(bf16[12,32,256]{2,1,0:T(8,128)(2,1)S(1)} %broadcast_in_dim.27), channel_id=1, replica_groups=mesh['y2'=2,'y1'=2,'x'=4,'core'=2,'yhi'=2,'z'=12] {'z'}, dimensions={0} | all-to-all | bytes 393216 | tf_op jit(solution)/shard_map/all_to_all | solution.py:78
  141.8 0.6 add_bitcast_fusion
  (6 shorter events, 0.1 us)
Async XLA Ops:
  0.0 0.8 copy-start.2
  0.0 0.8 copy-start.4
  0.0 0.8 copy-start.5
  0.8 0.8 copy-start.3
  30.0 2.5 %copy-start = (bf16[576,768]{1,0:T(8,128)(2,1)S(1)}, bf16[576,768]{1,0:T(8,128)(2,1)}, u32[]{:S(2)}) copy-start(bf16[576,768]{1,0:T(8,128)(2,1)} %screened_ref.3) | copy-start | bytes 2654212
  30.0 2.5 %copy-start.1 = (bf16[576,256]{1,0:T(8,128)(2,1)S(1)}, bf16[576,256]{1,0:T(8,128)(2,1)}, u32[]{:S(2)}) copy-start(bf16[576,256]{1,0:T(8,128)(2,1)} %val_ref.3) | copy-start | bytes 884740

commit v4 on v3

--- a/solution.py
+++ b/solution.py
@@ -10,7 +10,8 @@
 BF16 = jnp.bfloat16
 
 ROW = ("y2", "y1", "x", "core")
-COL = ("yhi", "z")
+COL = ("yhi", "z3", "za", "zb")
+RING = ("zb", "za", "z3")
 NEAR = ("y1", "x")
 PLANE = ("y1", "x", "y2")
 WIDE = ("y1", "x", "y2", "yhi")
@@ -18,11 +19,28 @@
 VMEM = pl.BlockSpec(memory_space=pltpu.VMEM)
 
 
-def start_kernel(offset_ref, trial_ref, cond_ref, val_ref, levels_ref, mine_ref, energy_ref):
-    width, n_cols = cond_ref.shape
-    lanes = levels_ref.shape[1]
+def start_kernel(trial_ref, cond_ref, mine_ref):
+    n_cols = cond_ref.shape[1]
     mine_ref[:, :n_cols] = cond_ref[...]
     mine_ref[:, n_cols:] = trial_ref[...].astype(BF16)
+
+
+def start(trial, cond):
+    width, n_cols = cond.shape
+    nv = trial.shape[1]
+    return pl.pallas_call(
+        start_kernel,
+        out_shape=jax.ShapeDtypeStruct((width, n_cols + nv), BF16),
+        in_specs=[VMEM, VMEM],
+        out_specs=VMEM,
+        compiler_params=pltpu.CompilerParams(vmem_limit_bytes=1 << 20),
+        name="start",
+    )(trial, cond)
+
+
+def energy_kernel(offset_ref, val_ref, levels_ref, energy_ref):
+    width = energy_ref.shape[0]
+    lanes = levels_ref.shape[1]
     offset = offset_ref[0]
     group = levels_ref[pl.ds(offset // lanes, 1), :]
     lane = lax.broadcasted_iota(jnp.int32, (width, lanes), 1)
@@ -31,21 +49,17 @@
     energy_ref[...] = jnp.sum(picked, axis=1, keepdims=True) - val_ref[...]
 
 
-def start(offset, trial, cond, eps_val, eps_cond):
-    width, n_cols = cond.shape
-    nv = trial.shape[1]
+def energies(offset, width, eps_val, eps_cond):
+    nv = eps_val.shape[0]
     lanes = 128
     return pl.pallas_call(
-        start_kernel,
-        out_shape=(
-            jax.ShapeDtypeStruct((width, n_cols + nv), BF16),
-            jax.ShapeDtypeStruct((width, nv), F32),
-        ),
-        in_specs=[pl.BlockSpec(memory_space=pltpu.SMEM), VMEM, VMEM, VMEM, VMEM],
-        out_specs=(VMEM, VMEM),
+        energy_kernel,
+        out_shape=jax.ShapeDtypeStruct((width, nv), F32),
+        in_specs=[pl.BlockSpec(memory_space=pltpu.SMEM), VMEM, VMEM],
+        out_specs=VMEM,
         compiler_params=pltpu.CompilerParams(vmem_limit_bytes=1 << 20),
-        name="start",
-    )(offset, trial, cond, eps_val.reshape(1, nv), eps_cond.reshape(-1, lanes))
+        name="energy",
+    )(offset, eps_val.reshape(1, nv), eps_cond.reshape(-1, lanes))
 
 
 def tile_kernel(both_ref, val_ref, screened_ref, out_ref, tile):
@@ -97,13 +111,15 @@
     half = width // 2
 
     x_mine = trial[0].T
+    mine = start(x_mine, cond_points.T)
     offset = (lax.axis_index(ROW) * width).reshape(1)
-    mine, energy = start(offset, x_mine, cond_points.T, eps_val, eps_cond)
     piece = lax.convert_element_type(lax.axis_index("yhi") * half, jnp.uint32)
     own = lax.convert_element_type(lax.axis_index(PLANE) * width, jnp.uint32)
-    mine, energy, piece, own = lax.optimization_barrier((mine, energy, piece, own))
+    mine, offset, piece, own = lax.optimization_barrier((mine, offset, piece, own))
     two = lax.all_gather(mine, "y2", axis=0, tiled=False)
     everything = copies_from_all(two, NEAR).reshape(blocks * width, n_cols + nv)
+    everything, eps_val, eps_cond = lax.optimization_barrier((everything, eps_val, eps_cond))
+    energy = energies(offset, width, eps_val, eps_cond)
     cond_half = everything[:, :n_cols]
     x_half = everything[:, n_cols:]
 
@@ -121,20 +137,20 @@
     for _ in range(APPLY - 1):
         terms = terms_of(x_half).reshape(2 * blocks, half, nv)
         rows = sent_and_summed(terms, WIDE)
-        x_piece = energy_piece * x_piece + summed_over_copies(rows.astype(BF16), "z")
+        x_piece = energy_piece * x_piece + summed_over_copies(rows.astype(BF16), RING)
         x_half = copies_from_all(x_piece.astype(BF16), WIDE).reshape(blocks * width, nv)
 
     terms = terms_of(x_half).reshape(blocks, 1, width, nv)
     twice = jnp.broadcast_to(terms, (blocks, 2, width, nv)).reshape(2 * blocks, width, nv)
     rows = sent_and_summed(twice, WIDE)
     x_mine = rows_from(x_half, own, width)
-    x_mine = energy * x_mine.astype(F32) + summed_over_copies(rows.astype(BF16), "z")
+    x_mine = energy * x_mine.astype(F32) + summed_over_copies(rows.astype(BF16), RING)
     return x_mine.T[None]
 
 
 def solution(mesh):
-    devices = mesh.devices.reshape(2, 2, 4, 2, 2, 12)
-    fine = Mesh(devices, ("y2", "y1", "x", "core", "yhi", "z"))
+    devices = mesh.devices.reshape(2, 2, 4, 2, 2, 3, 2, 2)
+    fine = Mesh(devices, ("y2", "y1", "x", "core", "yhi", "z3", "za", "zb"))
     in_specs = (P(None, None, ROW), P(ROW, COL), P(ROW, None), P(COL, ROW), P(), P())
     out_specs = P(None, None, ROW)
     return jax.shard_map(body, mesh=fine, in_specs=in_specs, out_specs=out_specs, check_vma=False)

time: 143 us -> 143 us (level)
  blocking collectives: 137 us -> 110 us
  starting transfers between devices: 0 us -> 15.3 us
  waiting for transfers between devices: 0 us -> 9.87 us
    all_to_all x4 -> x3, blocking collectives: 79.5 us -> 53.3 us  [copies_from_all(): return lax.all_to_all(copies, axes, 0, 0, tiled=True)]
    all_to_all x0 -> x1, starting transfers between devices: none -> 15.3 us  [copies_from_all(): return lax.all_to_all(copies, axes, 0, 0, tiled=True)]
    all_to_all x0 -> x1, waiting for transfers between devices: none -> 9.87 us  [copies_from_all(): return lax.all_to_all(copies, axes, 0, 0, tiled=True)]
  transfers between devices with their start and end apart: 0 -> 1, of which waited for: 0 -> 1; matrix products, arithmetic and copies ran while one was open for 0% -> 0% of each run, Pallas kernels for 0% -> 0%
where the time goes in v4:
time: 143 us
  blocking collectives  110 us (77%)
  starting transfers between devices  15.3 us (11%)
  waiting for transfers between devices  9.87 us (7%)
  local copies, waits for them, and re-layouts  3.07 us (2%)
  matrix products  1.61 us (1%)
  Pallas kernels  1.55 us (1%)
    all_to_all x3, blocking collectives, copies_from_all(): return lax.all_to_all(copies, axes, 0, 0, tiled=True)  53.3 us
    all_to_all x2, blocking collectives, sent_and_summed(): lax.all_to_all(blocks, axes, 0, 0, tiled=True).astype(F32)  41.6 us
    all_to_all x1, starting transfers between devices, copies_from_all(): return lax.all_to_all(copies, axes, 0, 0, tiled=True)  15.3 us
    all_to_all x1, waiting for transfers between devices, copies_from_all(): return lax.all_to_all(copies, axes, 0, 0, tiled=True)  9.87 us
    all_gather x1, blocking collectives, body(): two = lax.all_gather(mine, 'y2', axis=0, tiled=False)  5.82 us
    all_gather x2, blocking collectives, terms_of(): both = lax.all_gather(mixed_part.astype(BF16), 'core', axis=0, tiled=False)  4.87 us
    all_gather x2, blocking collectives, terms_of(): both = lax.all_gather(folded_part, 'core', axis=0, tiled=False)  4.74 us
  transfers between devices with their start and end apart: 1, of which 1 were waited for; matrix products, arithmetic and copies ran while one was open for 0% of the time, Pallas kernels for 0%

profile of v4, /device:TPU:8, one launch (start us, length us, event | category | flops | bytes accessed | tf_op | source)
XLA Modules:
  0.0 142.7 jit_solution(14864914642885164383)
XLA Ops:
  0.0 0.0 copy-start.2
  0.0 0.8 copy-done.2
  0.8 0.0 copy-start.3
  0.8 0.8 copy-done.3
  1.6 5.8 %all-gather = bf16[64,1024]{1,0:T(8,128)(2,1)S(1)} all-gather(bf16[32,1024]{1,0:T(8,128)(2,1)S(1)} %start.1), channel_id=2, replica_groups=mesh['y2'=2,'y1'=2,'x'=4,'core'=2,'yhi'=2,'z3'=3,'za'=2,'zb'=2] {'y2'}, dimensions={0}, use_global_device_ids=true | all-gather | bytes 196608 | tf_op jit(solution)/shard_map/all_gather | solution.py:119
  7.4 0.1 broadcast_in_dim.22
  7.5 22.0 %all_to_all.30 = bf16[8,2,32,1024]{3,2,1,0:T(8,128)(2,1)S(1)} all-to-all(bf16[8,2,32,1024]{3,2,1,0:T(8,128)(2,1)S(1)} %broadcast_in_dim.22), channel_id=1, replica_groups=mesh['y2'=2,'y1'=2,'x'=4,'core'=2,'yhi'=2,'z3'=3,'za'=2,'zb'=2] {'y1','x'}, dimensions={0} | all-to-all | bytes 2097152 | tf_op jit(solution)/shard_map/all_to_all | solution.py:92
  29.5 0.4 convolution_convert_fusion.1
  29.9 0.0 copy-start
  29.9 0.0 copy-start.1
  29.9 2.5 %all-gather.1.both_ref = bf16[512,768]{1,0:T(8,128)(2,1)S(1)} all-gather(bf16[256,768]{1,0:T(8,128)(2,1)S(1)} %convolution_convert_fusion.1), channel_id=3, replica_groups=mesh['y2'=2,'y1'=2,'x'=4,'core'=2,'yhi'=2,'z3'=3,'za'=2,'zb'=2] {'core'}, dimensions={0}, use_global_device_ids=true | all-gather | bytes 1179648 | tf_op jit(solution)/shard_map/all_gather | solution.py:128
  32.4 0.0 copy-done
  32.4 0.0 copy-done.1
  32.4 0.7 tile.2
  33.2 2.4 %all-gather.2 = bf16[512,768]{1,0:T(8,128)(2,1)S(1)} all-gather(bf16[256,768]{1,0:T(8,128)(2,1)S(1)} %tile.2), channel_id=4, replica_groups=mesh['y2'=2,'y1'=2,'x'=4,'core'=2,'yhi'=2,'z3'=3,'za'=2,'zb'=2] {'core'}, dimensions={0}, use_global_device_ids=true | all-gather | bytes 1179648 | tf_op jit(solution)/shard_map/all_gather | solution.py:130
  35.5 0.4 convolution_convert_fusion.3
  36.0 19.3 %all_to_all.31 = bf16[32,16,256]{2,1,0:T(8,128)(2,1)S(1)} all-to-all(bf16[32,16,256]{2,1,0:T(8,128)(2,1)S(1)} %bitcast.39), channel_id=1, replica_groups=mesh['y2'=2,'y1'=2,'x'=4,'core'=2,'yhi'=2,'z3'=3,'za'=2,'zb'=2] {'y1','x..., dimensions={0} | all-to-all | bytes 524288 | tf_op jit(solution)/shard_map/all_to_all | solution.py:100
  55.2 0.1 reduce_sum.42
  55.3 0.6 broadcast_in_dim.23
  55.9 0.0 copy-start.4
  55.9 15.3 %all-to-all-start.2 = ((bf16[12,16,256]{2,1,0:T(8,128)(2,1)}), bf16[12,16,256]{2,1,0:T(8,128)(2,1)S(1)}, u32[]{:S(2)}, u32[]{:S(2)}) async-start(bf16[12,16,256]{2,1,0:T(8,128)(2,1)} %broadcast_in_dim.23), calls=%async_computation.2 | async-start | bytes 196608 | tf_op jit(solution)/shard_map/all_to_all | solution.py:92
  71.2 0.0 copy-start.5
  71.2 0.0 copy-done.4
  71.2 0.7 copy-done.5
  71.9 0.1 energy.1
  72.0 9.9 %all-to-all-done.2 = bf16[12,16,256]{2,1,0:T(8,128)(2,1)S(1)} async-done(((bf16[12,16,256]{2,1,0:T(8,128)(2,1)}), bf16[12,16,256]{2,1,0:T(8,128)(2,1)S(1)}, u32[]{:S(2)}, u32[]{:S(2)}) %all-to-all-start.2) | async-done | bytes 98336 | tf_op jit(solution)/shard_map/all_to_all | solution.py:92
  81.9 14.8 %all_to_all.32 = bf16[32,16,256]{2,1,0:T(8,128)(2,1)S(1)} all-to-all(bf16[32,16,256]{2,1,0:T(8,128)(2,1)S(1)} %broadcast_in_dim.24), channel_id=1, replica_groups=mesh['y2'=2,'y1'=2,'x'=4,'core'=2,'yhi'=2,'z3'=3,'za'=2,'zb'=2] {'y1','x..., dimensions={0} | all-to-all | bytes 524288 | tf_op jit(solution)/shard_map/all_to_all | solution.py:92
  96.7 0.4 convolution_convert_fusion
  97.1 2.4 %all-gather.3.both_ref = bf16[512,768]{1,0:T(8,128)(2,1)S(1)} all-gather(bf16[256,768]{1,0:T(8,128)(2,1)S(1)} %convolution_convert_fusion), channel_id=5, replica_groups=mesh['y2'=2,'y1'=2,'x'=4,'core'=2,'yhi'=2,'z3'=3,'za'=2,'zb'=2] {'core'}, dimensions={0}, use_global_device_ids=true | all-gather | bytes 1179648 | tf_op jit(solution)/shard_map/all_gather | solution.py:128
  99.5 0.7 tile.3
  100.2 2.4 %all-gather.4 = bf16[512,768]{1,0:T(8,128)(2,1)S(1)} all-gather(bf16[256,768]{1,0:T(8,128)(2,1)S(1)} %tile.3), channel_id=6, replica_groups=mesh['y2'=2,'y1'=2,'x'=4,'core'=2,'yhi'=2,'z3'=3,'za'=2,'zb'=2] {'core'}, dimensions={0}, use_global_device_ids=true | all-gather | bytes 1179648 | tf_op jit(solution)/shard_map/all_gather | solution.py:130
  102.6 0.4 convolution_convert_fusion.2
  103.0 0.1 broadcast_in_dim.26
  103.1 22.3 %all_to_all.33 = bf16[32,32,256]{2,1,0:T(8,128)(2,1)S(1)} all-to-all(bf16[32,32,256]{2,1,0:T(8,128)(2,1)S(1)} %bitcast.30), channel_id=1, replica_groups=mesh['y2'=2,'y1'=2,'x'=4,'core'=2,'yhi'=2,'z3'=3,'za'=2,'zb'=2] {'y1','x..., dimensions={0} | all-to-all | bytes 1048576 | tf_op jit(solution)/shard_map/all_to_all | solution.py:100
  125.4 0.1 reduce_sum.44
  125.5 16.5 %all_to_all.34 = bf16[12,32,256]{2,1,0:T(8,128)(2,1)S(1)} all-to-all(bf16[12,32,256]{2,1,0:T(8,128)(2,1)S(1)} %broadcast_in_dim.27), channel_id=1, replica_groups=mesh['y2'=2,'y1'=2,'x'=4,'core'=2,'yhi'=2,'z3'=3,'za'=2,'zb'=2] {'zb','z..., dimensions={0} | all-to-all | bytes 393216 | tf_op jit(solution)/shard_map/all_to_all | solution.py:92
  142.1 0.6 add_bitcast_fusion
  (6 shorter events, 0.1 us)
Async XLA Ops:
  0.0 0.8 copy-start.2
  0.8 0.8 copy-start.3
  29.9 2.5 %copy-start = (bf16[576,768]{1,0:T(8,128)(2,1)S(1)}, bf16[576,768]{1,0:T(8,128)(2,1)}, u32[]{:S(2)}) copy-start(bf16[576,768]{1,0:T(8,128)(2,1)} %screened_ref.3) | copy-start | bytes 2654212
  29.9 2.5 %copy-start.1 = (bf16[576,256]{1,0:T(8,128)(2,1)S(1)}, bf16[576,256]{1,0:T(8,128)(2,1)}, u32[]{:S(2)}) copy-start(bf16[576,256]{1,0:T(8,128)(2,1)} %val_ref.3) | copy-start | bytes 884740
  55.9 15.3 %copy-start.4 = (f32[1024]{0:T(1024)S(1)}, f32[1024]{0:T(1024)}, u32[]{:S(2)}) copy-start(f32[1024]{0:T(1024)} %param.11) | copy-start | bytes 12292
  55.9 25.9 %all-to-all-start.2 = ((bf16[12,16,256]{2,1,0:T(8,128)(2,1)}), bf16[12,16,256]{2,1,0:T(8,128)(2,1)S(1)}, u32[]{:S(2)}, u32[]{:S(2)}) async-start(bf16[12,16,256]{2,1,0:T(8,128)(2,1)} %broadcast_in_dim.23), calls=%async_computation.2 | async-start | bytes 196608 | tf_op jit(solution)/shard_map/all_to_all | solution.py:92
  71.2 0.7 copy-start.5

commit v5 on v3

--- a/solution.py
+++ b/solution.py
@@ -10,17 +10,25 @@
 BF16 = jnp.bfloat16
 
 ROW = ("y2", "y1", "x", "core")
-COL = ("yhi", "z")
+COL = ("yhi", "z3", "za", "zb")
+RING = ("zb", "za", "z3")
 NEAR = ("y1", "x")
 PLANE = ("y1", "x", "y2")
 WIDE = ("y1", "x", "y2", "yhi")
 
 VMEM = pl.BlockSpec(memory_space=pltpu.VMEM)
+HBM = pl.BlockSpec(memory_space=pltpu.HBM)
 
 
-def start_kernel(offset_ref, trial_ref, cond_ref, val_ref, levels_ref, mine_ref, energy_ref):
+def start_kernel(offset_ref, trial_hbm, cond_hbm, val_hbm, levels_hbm, mine_ref, energy_ref, trial_ref, cond_ref, val_ref, levels_ref, sems):
     width, n_cols = cond_ref.shape
     lanes = levels_ref.shape[1]
+    pairs = ((cond_hbm, cond_ref), (trial_hbm, trial_ref), (levels_hbm, levels_ref), (val_hbm, val_ref))
+    copies = [pltpu.make_async_copy(*pair, sems.at[k]) for k, pair in enumerate(pairs)]
+    for copy in copies:
+        copy.start()
+    for copy in copies:
+        copy.wait()
     mine_ref[:, :n_cols] = cond_ref[...]
     mine_ref[:, n_cols:] = trial_ref[...].astype(BF16)
     offset = offset_ref[0]
@@ -35,17 +43,20 @@
     width, n_cols = cond.shape
     nv = trial.shape[1]
     lanes = 128
+    operands = (trial, cond, eps_val.reshape(1, nv), eps_cond.reshape(-1, lanes))
+    operands = [pltpu.with_memory_space_constraint(x, pltpu.HBM) for x in operands]
     return pl.pallas_call(
         start_kernel,
         out_shape=(
-            jax.ShapeDtypeStruct((width, n_cols + nv), BF16),
-            jax.ShapeDtypeStruct((width, nv), F32),
+            pltpu.VMEM((width, n_cols + nv), BF16),
+            pltpu.VMEM((width, nv), F32),
         ),
-        in_specs=[pl.BlockSpec(memory_space=pltpu.SMEM), VMEM, VMEM, VMEM, VMEM],
+        in_specs=[pl.BlockSpec(memory_space=pltpu.SMEM), HBM, HBM, HBM, HBM],
         out_specs=(VMEM, VMEM),
+        scratch_shapes=[pltpu.VMEM(x.shape, x.dtype) for x in operands] + [pltpu.SemaphoreType.DMA((4,))],
         compiler_params=pltpu.CompilerParams(vmem_limit_bytes=1 << 20),
         name="start",
-    )(offset, trial, cond, eps_val.reshape(1, nv), eps_cond.reshape(-1, lanes))
+    )(offset, *operands)
 
 
 def tile_kernel(both_ref, val_ref, screened_ref, out_ref, tile):
@@ -121,20 +132,20 @@
     for _ in range(APPLY - 1):
         terms = terms_of(x_half).reshape(2 * blocks, half, nv)
         rows = sent_and_summed(terms, WIDE)
-        x_piece = energy_piece * x_piece + summed_over_copies(rows.astype(BF16), "z")
+        x_piece = energy_piece * x_piece + summed_over_copies(rows.astype(BF16), RING)
         x_half = copies_from_all(x_piece.astype(BF16), WIDE).reshape(blocks * width, nv)
 
     terms = terms_of(x_half).reshape(blocks, 1, width, nv)
     twice = jnp.broadcast_to(terms, (blocks, 2, width, nv)).reshape(2 * blocks, width, nv)
     rows = sent_and_summed(twice, WIDE)
     x_mine = rows_from(x_half, own, width)
-    x_mine = energy * x_mine.astype(F32) + summed_over_copies(rows.astype(BF16), "z")
+    x_mine = energy * x_mine.astype(F32) + summed_over_copies(rows.astype(BF16), RING)
     return x_mine.T[None]
 
 
 def solution(mesh):
-    devices = mesh.devices.reshape(2, 2, 4, 2, 2, 12)
-    fine = Mesh(devices, ("y2", "y1", "x", "core", "yhi", "z"))
+    devices = mesh.devices.reshape(2, 2, 4, 2, 2, 3, 2, 2)
+    fine = Mesh(devices, ("y2", "y1", "x", "core", "yhi", "z3", "za", "zb"))
     in_specs = (P(None, None, ROW), P(ROW, COL), P(ROW, None), P(COL, ROW), P(), P())
     out_specs = P(None, None, ROW)
     return jax.shard_map(body, mesh=fine, in_specs=in_specs, out_specs=out_specs, check_vma=False)

time: 143 us -> 142 us (level)
  no operation moved by 1% of the time
where the time goes in v5:
time: 142 us
  blocking collectives  136 us (96%)
  Pallas kernels  2.38 us (2%)
  matrix products  1.6 us (1%)
    all_to_all x4, blocking collectives, copies_from_all(): return lax.all_to_all(copies, axes, 0, 0, tiled=True)  78.9 us
    all_to_all x2, blocking collectives, sent_and_summed(): lax.all_to_all(blocks, axes, 0, 0, tiled=True).astype(F32)  41.6 us
    all_gather x1, blocking collectives, body(): two = lax.all_gather(mine, 'y2', axis=0, tiled=False)  5.83 us
    all_gather x2, blocking collectives, terms_of(): both = lax.all_gather(mixed_part.astype(BF16), 'core', axis=0, tiled=False)  4.87 us
    all_gather x2, blocking collectives, terms_of(): both = lax.all_gather(folded_part, 'core', axis=0, tiled=False)  4.74 us

profile of v5, /device:TPU:8, one launch (start us, length us, event | category | flops | bytes accessed | tf_op | source)
XLA Modules:
  0.0 141.8 jit_solution(11199137689275322553)
XLA Ops:
  0.0 0.9 start.1
  0.9 5.8 %all-gather = bf16[64,1024]{1,0:T(8,128)(2,1)S(1)} all-gather(bf16[32,1024]{1,0:T(8,128)(2,1)S(1)} %get-tuple-element.15), channel_id=2, replica_groups=mesh['y2'=2,'y1'=2,'x'=4,'core'=2,'yhi'=2,'z3'=3,'za'=2,'zb'=2] {'y2'}, dimensions={0}, use_global_device_ids=true | all-gather | bytes 196608 | tf_op jit(solution)/shard_map/all_gather | solution.py:116
  6.8 0.1 broadcast_in_dim.22
  6.9 22.0 %all_to_all.30 = bf16[8,2,32,1024]{3,2,1,0:T(8,128)(2,1)S(1)} all-to-all(bf16[8,2,32,1024]{3,2,1,0:T(8,128)(2,1)S(1)} %broadcast_in_dim.22), channel_id=1, replica_groups=mesh['y2'=2,'y1'=2,'x'=4,'core'=2,'yhi'=2,'z3'=3,'za'=2,'zb'=2] {'y1','x'}, dimensions={0} | all-to-all | bytes 2097152 | tf_op jit(solution)/shard_map/all_to_all | solution.py:89
  28.9 0.4 convolution_convert_fusion.1
  29.3 0.0 copy-start
  29.3 0.0 copy-start.1
  29.3 2.5 %all-gather.1.both_ref = bf16[512,768]{1,0:T(8,128)(2,1)S(1)} all-gather(bf16[256,768]{1,0:T(8,128)(2,1)S(1)} %convolution_convert_fusion.1), channel_id=3, replica_groups=mesh['y2'=2,'y1'=2,'x'=4,'core'=2,'yhi'=2,'z3'=3,'za'=2,'zb'=2] {'core'}, dimensions={0}, use_global_device_ids=true | all-gather | bytes 1179648 | tf_op jit(solution)/shard_map/all_gather | solution.py:123
  31.8 0.0 copy-done
  31.8 0.0 copy-done.1
  31.8 0.7 tile.2
  32.5 2.4 %all-gather.2 = bf16[512,768]{1,0:T(8,128)(2,1)S(1)} all-gather(bf16[256,768]{1,0:T(8,128)(2,1)S(1)} %tile.2), channel_id=4, replica_groups=mesh['y2'=2,'y1'=2,'x'=4,'core'=2,'yhi'=2,'z3'=3,'za'=2,'zb'=2] {'core'}, dimensions={0}, use_global_device_ids=true | all-gather | bytes 1179648 | tf_op jit(solution)/shard_map/all_gather | solution.py:125
  34.9 0.4 convolution_convert_fusion.3
  35.3 19.3 %all_to_all.31 = bf16[32,16,256]{2,1,0:T(8,128)(2,1)S(1)} all-to-all(bf16[32,16,256]{2,1,0:T(8,128)(2,1)S(1)} %bitcast.35), channel_id=1, replica_groups=mesh['y2'=2,'y1'=2,'x'=4,'core'=2,'yhi'=2,'z3'=3,'za'=2,'zb'=2] {'y1','x..., dimensions={0} | all-to-all | bytes 524288 | tf_op jit(solution)/shard_map/all_to_all | solution.py:97
  54.6 0.1 reduce_sum.42
  54.7 25.6 %all_to_all.32 = bf16[12,16,256]{2,1,0:T(8,128)(2,1)S(1)} all-to-all(bf16[12,16,256]{2,1,0:T(8,128)(2,1)S(1)} %broadcast_in_dim.23), channel_id=1, replica_groups=mesh['y2'=2,'y1'=2,'x'=4,'core'=2,'yhi'=2,'z3'=3,'za'=2,'zb'=2] {'zb','z..., dimensions={0} | all-to-all | bytes 196608 | tf_op jit(solution)/shard_map/all_to_all | solution.py:89
  80.3 0.0 copy-start.2
  80.3 0.7 copy-done.2
  81.1 14.8 %all_to_all.33 = bf16[32,16,256]{2,1,0:T(8,128)(2,1)S(1)} all-to-all(bf16[32,16,256]{2,1,0:T(8,128)(2,1)S(1)} %broadcast_in_dim.24), channel_id=1, replica_groups=mesh['y2'=2,'y1'=2,'x'=4,'core'=2,'yhi'=2,'z3'=3,'za'=2,'zb'=2] {'y1','x..., dimensions={0} | all-to-all | bytes 524288 | tf_op jit(solution)/shard_map/all_to_all | solution.py:89
  95.9 0.4 convolution_convert_fusion
  96.3 2.4 %all-gather.3.both_ref = bf16[512,768]{1,0:T(8,128)(2,1)S(1)} all-gather(bf16[256,768]{1,0:T(8,128)(2,1)S(1)} %convolution_convert_fusion), channel_id=5, replica_groups=mesh['y2'=2,'y1'=2,'x'=4,'core'=2,'yhi'=2,'z3'=3,'za'=2,'zb'=2] {'core'}, dimensions={0}, use_global_device_ids=true | all-gather | bytes 1179648 | tf_op jit(solution)/shard_map/all_gather | solution.py:123
  98.7 0.7 tile.3
  99.4 2.4 %all-gather.4 = bf16[512,768]{1,0:T(8,128)(2,1)S(1)} all-gather(bf16[256,768]{1,0:T(8,128)(2,1)S(1)} %tile.3), channel_id=6, replica_groups=mesh['y2'=2,'y1'=2,'x'=4,'core'=2,'yhi'=2,'z3'=3,'za'=2,'zb'=2] {'core'}, dimensions={0}, use_global_device_ids=true | all-gather | bytes 1179648 | tf_op jit(solution)/shard_map/all_gather | solution.py:125
  101.8 0.4 convolution_convert_fusion.2
  102.2 0.1 broadcast_in_dim.26
  102.2 22.3 %all_to_all.34 = bf16[32,32,256]{2,1,0:T(8,128)(2,1)S(1)} all-to-all(bf16[32,32,256]{2,1,0:T(8,128)(2,1)S(1)} %bitcast.26), channel_id=1, replica_groups=mesh['y2'=2,'y1'=2,'x'=4,'core'=2,'yhi'=2,'z3'=3,'za'=2,'zb'=2] {'y1','x..., dimensions={0} | all-to-all | bytes 1048576 | tf_op jit(solution)/shard_map/all_to_all | solution.py:97
  124.6 0.1 reduce_sum.44
  124.7 16.5 %all_to_all.35 = bf16[12,32,256]{2,1,0:T(8,128)(2,1)S(1)} all-to-all(bf16[12,32,256]{2,1,0:T(8,128)(2,1)S(1)} %broadcast_in_dim.27), channel_id=1, replica_groups=mesh['y2'=2,'y1'=2,'x'=4,'core'=2,'yhi'=2,'z3'=3,'za'=2,'zb'=2] {'zb','z..., dimensions={0} | all-to-all | bytes 393216 | tf_op jit(solution)/shard_map/all_to_all | solution.py:89
  141.2 0.6 add_bitcast_fusion
  (6 shorter events, 0.1 us)
Async XLA Ops:
  29.3 2.5 %copy-start = (bf16[576,768]{1,0:T(8,128)(2,1)S(1)}, bf16[576,768]{1,0:T(8,128)(2,1)}, u32[]{:S(2)}) copy-start(bf16[576,768]{1,0:T(8,128)(2,1)} %screened_ref.3) | copy-start | bytes 2654212
  29.3 2.5 %copy-start.1 = (bf16[576,256]{1,0:T(8,128)(2,1)S(1)}, bf16[576,256]{1,0:T(8,128)(2,1)}, u32[]{:S(2)}) copy-start(bf16[576,256]{1,0:T(8,128)(2,1)} %val_ref.3) | copy-start | bytes 884740
  80.3 0.8 copy-start.2

commit v6 on v5

--- a/solution.py
+++ b/solution.py
@@ -135,11 +135,12 @@
         x_piece = energy_piece * x_piece + summed_over_copies(rows.astype(BF16), RING)
         x_half = copies_from_all(x_piece.astype(BF16), WIDE).reshape(blocks * width, nv)
 
-    terms = terms_of(x_half).reshape(blocks, 1, width, nv)
-    twice = jnp.broadcast_to(terms, (blocks, 2, width, nv)).reshape(2 * blocks, width, nv)
-    rows = sent_and_summed(twice, WIDE)
+    terms = terms_of(x_half).reshape(blocks, width, nv)
+    rows = sent_and_summed(terms, PLANE)
     x_mine = rows_from(x_half, own, width)
-    x_mine = energy * x_mine.astype(F32) + summed_over_copies(rows.astype(BF16), RING)
+    along = summed_over_copies(rows.astype(BF16), RING).astype(BF16)
+    both = lax.all_gather(along, "yhi", axis=0, tiled=False)
+    x_mine = energy * x_mine.astype(F32) + (both[0].astype(F32) + both[1].astype(F32))
     return x_mine.T[None]
 
 

time: 142 us -> 141 us (level)
  the two profiles are of different devices: /device:TPU:8 before, /device:TPU:56 now
where the time goes in v6:
time: 141 us; the launch traced here: 140 us
  blocking collectives  134 us (95%)
  Pallas kernels  2.38 us (2%)
  matrix products  1.6 us (1%)
    all_to_all x4, blocking collectives, copies_from_all(): return lax.all_to_all(copies, axes, 0, 0, tiled=True)  75.2 us
    all_to_all x2, blocking collectives, sent_and_summed(): lax.all_to_all(blocks, axes, 0, 0, tiled=True).astype(F32)  34.2 us
    all_gather x1, blocking collectives, body(): both = lax.all_gather(along, 'yhi', axis=0, tiled=False)  8.32 us
    all_gather x1, blocking collectives, body(): two = lax.all_gather(mine, 'y2', axis=0, tiled=False)  6.88 us
    all_gather x2, blocking collectives, terms_of(): both = lax.all_gather(mixed_part.astype(BF16), 'core', axis=0, tiled=False)  4.87 us
    all_gather x2, blocking collectives, terms_of(): both = lax.all_gather(folded_part, 'core', axis=0, tiled=False)  4.74 us

profile of v6, /device:TPU:56, one launch (start us, length us, event | category | flops | bytes accessed | tf_op | source)
XLA Modules:
  0.0 140.0 jit_solution(3379649925298707699)
XLA Ops:
  0.0 0.9 start.1
  0.9 6.9 %all-gather = bf16[64,1024]{1,0:T(8,128)(2,1)S(1)} all-gather(bf16[32,1024]{1,0:T(8,128)(2,1)S(1)} %get-tuple-element.15), channel_id=2, replica_groups=mesh['y2'=2,'y1'=2,'x'=4,'core'=2,'yhi'=2,'z3'=3,'za'=2,'zb'=2] {'y2'}, dimensions={0}, use_global_device_ids=true | all-gather | bytes 196608 | tf_op jit(solution)/shard_map/all_gather | solution.py:116
  7.8 0.1 broadcast_in_dim.15
  7.9 18.3 %all_to_all.30 = bf16[8,2,32,1024]{3,2,1,0:T(8,128)(2,1)S(1)} all-to-all(bf16[8,2,32,1024]{3,2,1,0:T(8,128)(2,1)S(1)} %broadcast_in_dim.15), channel_id=1, replica_groups=mesh['y2'=2,'y1'=2,'x'=4,'core'=2,'yhi'=2,'z3'=3,'za'=2,'zb'=2] {'y1','x'}, dimensions={0} | all-to-all | bytes 2097152 | tf_op jit(solution)/shard_map/all_to_all | solution.py:89
  26.2 0.4 convolution_convert_fusion.1
  26.6 0.0 copy-start
  26.6 0.0 copy-start.1
  26.7 2.5 %all-gather.1.both_ref = bf16[512,768]{1,0:T(8,128)(2,1)S(1)} all-gather(bf16[256,768]{1,0:T(8,128)(2,1)S(1)} %convolution_convert_fusion.1), channel_id=3, replica_groups=mesh['y2'=2,'y1'=2,'x'=4,'core'=2,'yhi'=2,'z3'=3,'za'=2,'zb'=2] {'core'}, dimensions={0}, use_global_device_ids=true | all-gather | bytes 1179648 | tf_op jit(solution)/shard_map/all_gather | solution.py:123
  29.2 0.0 copy-done
  29.2 0.0 copy-done.1
  29.2 0.7 tile.2
  29.9 2.4 %all-gather.2 = bf16[512,768]{1,0:T(8,128)(2,1)S(1)} all-gather(bf16[256,768]{1,0:T(8,128)(2,1)S(1)} %tile.2), channel_id=4, replica_groups=mesh['y2'=2,'y1'=2,'x'=4,'core'=2,'yhi'=2,'z3'=3,'za'=2,'zb'=2] {'core'}, dimensions={0}, use_global_device_ids=true | all-gather | bytes 1179648 | tf_op jit(solution)/shard_map/all_gather | solution.py:125
  32.3 0.4 convolution_convert_fusion.3
  32.7 18.9 %all_to_all.31 = bf16[32,16,256]{2,1,0:T(8,128)(2,1)S(1)} all-to-all(bf16[32,16,256]{2,1,0:T(8,128)(2,1)S(1)} %bitcast.33), channel_id=1, replica_groups=mesh['y2'=2,'y1'=2,'x'=4,'core'=2,'yhi'=2,'z3'=3,'za'=2,'zb'=2] {'y1','x..., dimensions={0} | all-to-all | bytes 524288 | tf_op jit(solution)/shard_map/all_to_all | solution.py:97
  51.6 0.1 reduce_sum.45
  51.7 25.6 %all_to_all.32 = bf16[12,16,256]{2,1,0:T(8,128)(2,1)S(1)} all-to-all(bf16[12,16,256]{2,1,0:T(8,128)(2,1)S(1)} %broadcast_in_dim.16), channel_id=1, replica_groups=mesh['y2'=2,'y1'=2,'x'=4,'core'=2,'yhi'=2,'z3'=3,'za'=2,'zb'=2] {'zb','z..., dimensions={0} | all-to-all | bytes 196608 | tf_op jit(solution)/shard_map/all_to_all | solution.py:89
  77.3 0.0 copy-start.2
  77.4 0.7 copy-done.2
  78.1 15.2 %all_to_all.33 = bf16[32,16,256]{2,1,0:T(8,128)(2,1)S(1)} all-to-all(bf16[32,16,256]{2,1,0:T(8,128)(2,1)S(1)} %broadcast_in_dim.17), channel_id=1, replica_groups=mesh['y2'=2,'y1'=2,'x'=4,'core'=2,'yhi'=2,'z3'=3,'za'=2,'zb'=2] {'y1','x..., dimensions={0} | all-to-all | bytes 524288 | tf_op jit(solution)/shard_map/all_to_all | solution.py:89
  93.4 0.4 convolution_convert_fusion
  93.7 2.4 %all-gather.3.both_ref = bf16[512,768]{1,0:T(8,128)(2,1)S(1)} all-gather(bf16[256,768]{1,0:T(8,128)(2,1)S(1)} %convolution_convert_fusion), channel_id=5, replica_groups=mesh['y2'=2,'y1'=2,'x'=4,'core'=2,'yhi'=2,'z3'=3,'za'=2,'zb'=2] {'core'}, dimensions={0}, use_global_device_ids=true | all-gather | bytes 1179648 | tf_op jit(solution)/shard_map/all_gather | solution.py:123
  96.1 0.7 tile.3
  96.9 2.4 %all-gather.4 = bf16[512,768]{1,0:T(8,128)(2,1)S(1)} all-gather(bf16[256,768]{1,0:T(8,128)(2,1)S(1)} %tile.3), channel_id=6, replica_groups=mesh['y2'=2,'y1'=2,'x'=4,'core'=2,'yhi'=2,'z3'=3,'za'=2,'zb'=2] {'core'}, dimensions={0}, use_global_device_ids=true | all-gather | bytes 1179648 | tf_op jit(solution)/shard_map/all_gather | solution.py:125
  99.2 0.4 convolution_convert_fusion.2
  99.6 15.3 %all_to_all.34 = bf16[16,32,256]{2,1,0:T(8,128)(2,1)S(1)} all-to-all(bf16[16,32,256]{2,1,0:T(8,128)(2,1)S(1)} %bitcast.32), channel_id=1, replica_groups=mesh['y2'=2,'y1'=2,'x'=4,'core'=2,'yhi'=2,'z3'=3,'za'=2,'zb'=2] {'y1','x..., dimensions={0} | all-to-all | bytes 524288 | tf_op jit(solution)/shard_map/all_to_all | solution.py:97
  115.0 16.0 %all_to_all.35 = bf16[12,32,256]{2,1,0:T(8,128)(2,1)S(1)} all-to-all(bf16[12,32,256]{2,1,0:T(8,128)(2,1)S(1)} %broadcast_in_dim.18), channel_id=1, replica_groups=mesh['y2'=2,'y1'=2,'x'=4,'core'=2,'yhi'=2,'z3'=3,'za'=2,'zb'=2] {'zb','z..., dimensions={0} | all-to-all | bytes 393216 | tf_op jit(solution)/shard_map/all_to_all | solution.py:89
  131.1 8.3 %all-gather.5 = bf16[64,256]{1,0:T(8,128)(2,1)S(1)} all-gather(bf16[32,256]{1,0:T(8,128)(2,1)S(1)} %reduce_sum.48), channel_id=7, replica_groups=mesh['y2'=2,'y1'=2,'x'=4,'core'=2,'yhi'=2,'z3'=3,'za'=2,'zb'=2] {'yhi'}, dimensions={0}, use_global_device_ids=true | all-gather | bytes 49152 | tf_op jit(solution)/shard_map/all_gather | solution.py:142
  139.4 0.6 fusion.9
  (7 shorter events, 0.2 us)
Async XLA Ops:
  26.6 2.5 %copy-start = (bf16[576,768]{1,0:T(8,128)(2,1)S(1)}, bf16[576,768]{1,0:T(8,128)(2,1)}, u32[]{:S(2)}) copy-start(bf16[576,768]{1,0:T(8,128)(2,1)} %screened_ref.3) | copy-start | bytes 2654212
  26.6 2.5 %copy-start.1 = (bf16[576,256]{1,0:T(8,128)(2,1)S(1)}, bf16[576,256]{1,0:T(8,128)(2,1)}, u32[]{:S(2)}) copy-start(bf16[576,256]{1,0:T(8,128)(2,1)} %val_ref.3) | copy-start | bytes 884740
  77.3 0.8 copy-start.2

commit v7 on v6

--- a/solution.py
+++ b/solution.py
@@ -27,9 +27,8 @@
     copies = [pltpu.make_async_copy(*pair, sems.at[k]) for k, pair in enumerate(pairs)]
     for copy in copies:
         copy.start()
-    for copy in copies:
+    for copy in copies[1:]:
         copy.wait()
-    mine_ref[:, :n_cols] = cond_ref[...]
     mine_ref[:, n_cols:] = trial_ref[...].astype(BF16)
     offset = offset_ref[0]
     group = levels_ref[pl.ds(offset // lanes, 1), :]
@@ -37,6 +36,8 @@
     row = lax.broadcasted_iota(jnp.int32, (width, lanes), 0)
     picked = jnp.where(lane == row + offset % lanes, group, 0.0)
     energy_ref[...] = jnp.sum(picked, axis=1, keepdims=True) - val_ref[...]
+    copies[0].wait()
+    mine_ref[:, :n_cols] = cond_ref[...]
 
 
 def start(offset, trial, cond, eps_val, eps_cond):
@@ -138,9 +139,9 @@
     terms = terms_of(x_half).reshape(blocks, width, nv)
     rows = sent_and_summed(terms, PLANE)
     x_mine = rows_from(x_half, own, width)
-    along = summed_over_copies(rows.astype(BF16), RING).astype(BF16)
-    both = lax.all_gather(along, "yhi", axis=0, tiled=False)
-    x_mine = energy * x_mine.astype(F32) + (both[0].astype(F32) + both[1].astype(F32))
+    both = lax.all_gather(rows.astype(BF16), "yhi", axis=0, tiled=False)
+    rows = both[0].astype(F32) + both[1].astype(F32)
+    x_mine = energy * x_mine.astype(F32) + summed_over_copies(rows.astype(BF16), RING)
     return x_mine.T[None]
 
 

time: 141 us -> 141 us (level)
  the two profiles are of different devices: /device:TPU:56 before, /device:TPU:2 now
where the time goes in v7:
time: 141 us; the launch traced here: 140 us
  blocking collectives  134 us (95%)
  Pallas kernels  2.37 us (2%)
  matrix products  1.6 us (1%)
    all_to_all x4, blocking collectives, copies_from_all(): return lax.all_to_all(copies, axes, 0, 0, tiled=True)  76.5 us
    all_to_all x2, blocking collectives, sent_and_summed(): lax.all_to_all(blocks, axes, 0, 0, tiled=True).astype(F32)  32.9 us
    all_gather x1, blocking collectives, body(): both = lax.all_gather(rows.astype(BF16), 'yhi', axis=0, tiled=False)  8.32 us
    all_gather x1, blocking collectives, body(): two = lax.all_gather(mine, 'y2', axis=0, tiled=False)  7.11 us
    all_gather x2, blocking collectives, terms_of(): both = lax.all_gather(mixed_part.astype(BF16), 'core', axis=0, tiled=False)  4.87 us
    all_gather x2, blocking collectives, terms_of(): both = lax.all_gather(folded_part, 'core', axis=0, tiled=False)  4.74 us

profile of v7, /device:TPU:2, one launch (start us, length us, event | category | flops | bytes accessed | tf_op | source)
XLA Modules:
  0.0 140.2 jit_solution(9286036327210948257)
XLA Ops:
  0.0 0.9 start.1
  0.9 7.1 %all-gather = bf16[64,1024]{1,0:T(8,128)(2,1)S(1)} all-gather(bf16[32,1024]{1,0:T(8,128)(2,1)S(1)} %get-tuple-element.15), channel_id=2, replica_groups=mesh['y2'=2,'y1'=2,'x'=4,'core'=2,'yhi'=2,'z3'=3,'za'=2,'zb'=2] {'y2'}, dimensions={0}, use_global_device_ids=true | all-gather | bytes 196608 | tf_op jit(solution)/shard_map/all_gather | solution.py:117
  8.0 0.1 broadcast_in_dim.15
  8.1 20.4 %all_to_all.30 = bf16[8,2,32,1024]{3,2,1,0:T(8,128)(2,1)S(1)} all-to-all(bf16[8,2,32,1024]{3,2,1,0:T(8,128)(2,1)S(1)} %broadcast_in_dim.15), channel_id=1, replica_groups=mesh['y2'=2,'y1'=2,'x'=4,'core'=2,'yhi'=2,'z3'=3,'za'=2,'zb'=2] {'y1','x'}, dimensions={0} | all-to-all | bytes 2097152 | tf_op jit(solution)/shard_map/all_to_all | solution.py:90
  28.5 0.4 convolution_convert_fusion.1
  28.9 0.0 copy-start
  29.0 0.0 copy-start.1
  29.0 2.5 %all-gather.1.both_ref = bf16[512,768]{1,0:T(8,128)(2,1)S(1)} all-gather(bf16[256,768]{1,0:T(8,128)(2,1)S(1)} %convolution_convert_fusion.1), channel_id=3, replica_groups=mesh['y2'=2,'y1'=2,'x'=4,'core'=2,'yhi'=2,'z3'=3,'za'=2,'zb'=2] {'core'}, dimensions={0}, use_global_device_ids=true | all-gather | bytes 1179648 | tf_op jit(solution)/shard_map/all_gather | solution.py:124
  31.5 0.0 copy-done
  31.5 0.0 copy-done.1
  31.5 0.7 tile.2
  32.2 2.4 %all-gather.2 = bf16[512,768]{1,0:T(8,128)(2,1)S(1)} all-gather(bf16[256,768]{1,0:T(8,128)(2,1)S(1)} %tile.2), channel_id=4, replica_groups=mesh['y2'=2,'y1'=2,'x'=4,'core'=2,'yhi'=2,'z3'=3,'za'=2,'zb'=2] {'core'}, dimensions={0}, use_global_device_ids=true | all-gather | bytes 1179648 | tf_op jit(solution)/shard_map/all_gather | solution.py:126
  34.6 0.4 convolution_convert_fusion.3
  35.0 18.9 %all_to_all.31 = bf16[32,16,256]{2,1,0:T(8,128)(2,1)S(1)} all-to-all(bf16[32,16,256]{2,1,0:T(8,128)(2,1)S(1)} %bitcast.33), channel_id=1, replica_groups=mesh['y2'=2,'y1'=2,'x'=4,'core'=2,'yhi'=2,'z3'=3,'za'=2,'zb'=2] {'y1','x..., dimensions={0} | all-to-all | bytes 524288 | tf_op jit(solution)/shard_map/all_to_all | solution.py:98
  53.9 0.1 reduce_sum.42
  53.9 25.4 %all_to_all.32 = bf16[12,16,256]{2,1,0:T(8,128)(2,1)S(1)} all-to-all(bf16[12,16,256]{2,1,0:T(8,128)(2,1)S(1)} %broadcast_in_dim.16), channel_id=1, replica_groups=mesh['y2'=2,'y1'=2,'x'=4,'core'=2,'yhi'=2,'z3'=3,'za'=2,'zb'=2] {'zb','z..., dimensions={0} | all-to-all | bytes 196608 | tf_op jit(solution)/shard_map/all_to_all | solution.py:90
  79.4 0.0 copy-start.2
  79.4 0.7 copy-done.2
  80.2 15.2 %all_to_all.33 = bf16[32,16,256]{2,1,0:T(8,128)(2,1)S(1)} all-to-all(bf16[32,16,256]{2,1,0:T(8,128)(2,1)S(1)} %broadcast_in_dim.17), channel_id=1, replica_groups=mesh['y2'=2,'y1'=2,'x'=4,'core'=2,'yhi'=2,'z3'=3,'za'=2,'zb'=2] {'y1','x..., dimensions={0} | all-to-all | bytes 524288 | tf_op jit(solution)/shard_map/all_to_all | solution.py:90
  95.3 0.4 convolution_convert_fusion
  95.7 2.4 %all-gather.3.both_ref = bf16[512,768]{1,0:T(8,128)(2,1)S(1)} all-gather(bf16[256,768]{1,0:T(8,128)(2,1)S(1)} %convolution_convert_fusion), channel_id=5, replica_groups=mesh['y2'=2,'y1'=2,'x'=4,'core'=2,'yhi'=2,'z3'=3,'za'=2,'zb'=2] {'core'}, dimensions={0}, use_global_device_ids=true | all-gather | bytes 1179648 | tf_op jit(solution)/shard_map/all_gather | solution.py:124
  98.1 0.7 tile.3
  98.8 2.4 %all-gather.4 = bf16[512,768]{1,0:T(8,128)(2,1)S(1)} all-gather(bf16[256,768]{1,0:T(8,128)(2,1)S(1)} %tile.3), channel_id=6, replica_groups=mesh['y2'=2,'y1'=2,'x'=4,'core'=2,'yhi'=2,'z3'=3,'za'=2,'zb'=2] {'core'}, dimensions={0}, use_global_device_ids=true | all-gather | bytes 1179648 | tf_op jit(solution)/shard_map/all_gather | solution.py:126
  101.2 0.4 convolution_convert_fusion.2
  101.6 14.0 %all_to_all.34 = bf16[16,32,256]{2,1,0:T(8,128)(2,1)S(1)} all-to-all(bf16[16,32,256]{2,1,0:T(8,128)(2,1)S(1)} %bitcast.32), channel_id=1, replica_groups=mesh['y2'=2,'y1'=2,'x'=4,'core'=2,'yhi'=2,'z3'=3,'za'=2,'zb'=2] {'y1','x..., dimensions={0} | all-to-all | bytes 524288 | tf_op jit(solution)/shard_map/all_to_all | solution.py:98
  115.7 8.3 %all-gather.5 = bf16[64,256]{1,0:T(8,128)(2,1)S(1)} all-gather(bf16[32,256]{1,0:T(8,128)(2,1)S(1)} %reduce_sum.44), channel_id=7, replica_groups=mesh['y2'=2,'y1'=2,'x'=4,'core'=2,'yhi'=2,'z3'=3,'za'=2,'zb'=2] {'yhi'}, dimensions={0}, use_global_device_ids=true | all-gather | bytes 49152 | tf_op jit(solution)/shard_map/all_gather | solution.py:142
  124.1 15.5 %all_to_all.35 = bf16[12,32,256]{2,1,0:T(8,128)(2,1)S(1)} all-to-all(bf16[12,32,256]{2,1,0:T(8,128)(2,1)S(1)} %broadcast_in_dim.18), channel_id=1, replica_groups=mesh['y2'=2,'y1'=2,'x'=4,'core'=2,'yhi'=2,'z3'=3,'za'=2,'zb'=2] {'zb','z..., dimensions={0} | all-to-all | bytes 393216 | tf_op jit(solution)/shard_map/all_to_all | solution.py:90
  139.6 0.6 add_bitcast_fusion
  (8 shorter events, 0.2 us)
Async XLA Ops:
  28.9 2.5 %copy-start = (bf16[576,768]{1,0:T(8,128)(2,1)S(1)}, bf16[576,768]{1,0:T(8,128)(2,1)}, u32[]{:S(2)}) copy-start(bf16[576,768]{1,0:T(8,128)(2,1)} %screened_ref.3) | copy-start | bytes 2654212
  29.0 2.5 %copy-start.1 = (bf16[576,256]{1,0:T(8,128)(2,1)S(1)}, bf16[576,256]{1,0:T(8,128)(2,1)}, u32[]{:S(2)}) copy-start(bf16[576,256]{1,0:T(8,128)(2,1)} %val_ref.3) | copy-start | bytes 884740
  79.4 0.8 copy-start.2

commit v8 on v6

--- a/solution.py
+++ b/solution.py
@@ -11,7 +11,7 @@
 
 ROW = ("y2", "y1", "x", "core")
 COL = ("yhi", "z3", "za", "zb")
-RING = ("zb", "za", "z3")
+RING = ("zb", "z3", "za")
 NEAR = ("y1", "x")
 PLANE = ("y1", "x", "y2")
 WIDE = ("y1", "x", "y2", "yhi")

time: 141 us -> 141 us (level)
  the two profiles are of different devices: /device:TPU:56 before, /device:TPU:8 now
where the time goes in v8:
time: 141 us
  blocking collectives  135 us (96%)
  Pallas kernels  2.38 us (2%)
  matrix products  1.6 us (1%)
    all_to_all x4, blocking collectives, copies_from_all(): return lax.all_to_all(copies, axes, 0, 0, tiled=True)  78.8 us
    all_to_all x2, blocking collectives, sent_and_summed(): lax.all_to_all(blocks, axes, 0, 0, tiled=True).astype(F32)  32.2 us
    all_gather x1, blocking collectives, body(): both = lax.all_gather(along, 'yhi', axis=0, tiled=False)  8.32 us
    all_gather x1, blocking collectives, body(): two = lax.all_gather(mine, 'y2', axis=0, tiled=False)  5.83 us
    all_gather x2, blocking collectives, terms_of(): both = lax.all_gather(mixed_part.astype(BF16), 'core', axis=0, tiled=False)  4.87 us
    all_gather x2, blocking collectives, terms_of(): both = lax.all_gather(folded_part, 'core', axis=0, tiled=False)  4.74 us

profile of v8, /device:TPU:8, one launch (start us, length us, event | category | flops | bytes accessed | tf_op | source)
XLA Modules:
  0.0 140.5 jit_solution(6496613779801828689)
XLA Ops:
  0.0 0.9 start.1
  0.9 5.8 %all-gather = bf16[64,1024]{1,0:T(8,128)(2,1)S(1)} all-gather(bf16[32,1024]{1,0:T(8,128)(2,1)S(1)} %get-tuple-element.15), channel_id=2, replica_groups=mesh['y2'=2,'y1'=2,'x'=4,'core'=2,'yhi'=2,'z3'=3,'za'=2,'zb'=2] {'y2'}, dimensions={0}, use_global_device_ids=true | all-gather | bytes 196608 | tf_op jit(solution)/shard_map/all_gather | solution.py:116
  6.8 0.1 broadcast_in_dim.15
  6.9 22.0 %all_to_all.30 = bf16[8,2,32,1024]{3,2,1,0:T(8,128)(2,1)S(1)} all-to-all(bf16[8,2,32,1024]{3,2,1,0:T(8,128)(2,1)S(1)} %broadcast_in_dim.15), channel_id=1, replica_groups=mesh['y2'=2,'y1'=2,'x'=4,'core'=2,'yhi'=2,'z3'=3,'za'=2,'zb'=2] {'y1','x'}, dimensions={0} | all-to-all | bytes 2097152 | tf_op jit(solution)/shard_map/all_to_all | solution.py:89
  28.9 0.4 convolution_convert_fusion.1
  29.3 0.0 copy-start
  29.3 0.0 copy-start.1
  29.3 2.5 %all-gather.1.both_ref = bf16[512,768]{1,0:T(8,128)(2,1)S(1)} all-gather(bf16[256,768]{1,0:T(8,128)(2,1)S(1)} %convolution_convert_fusion.1), channel_id=3, replica_groups=mesh['y2'=2,'y1'=2,'x'=4,'core'=2,'yhi'=2,'z3'=3,'za'=2,'zb'=2] {'core'}, dimensions={0}, use_global_device_ids=true | all-gather | bytes 1179648 | tf_op jit(solution)/shard_map/all_gather | solution.py:123
  31.8 0.0 copy-done
  31.8 0.0 copy-done.1
  31.8 0.7 tile.2
  32.5 2.4 %all-gather.2 = bf16[512,768]{1,0:T(8,128)(2,1)S(1)} all-gather(bf16[256,768]{1,0:T(8,128)(2,1)S(1)} %tile.2), channel_id=4, replica_groups=mesh['y2'=2,'y1'=2,'x'=4,'core'=2,'yhi'=2,'z3'=3,'za'=2,'zb'=2] {'core'}, dimensions={0}, use_global_device_ids=true | all-gather | bytes 1179648 | tf_op jit(solution)/shard_map/all_gather | solution.py:125
  34.9 0.4 convolution_convert_fusion.3
  35.3 19.3 %all_to_all.31 = bf16[32,16,256]{2,1,0:T(8,128)(2,1)S(1)} all-to-all(bf16[32,16,256]{2,1,0:T(8,128)(2,1)S(1)} %bitcast.33), channel_id=1, replica_groups=mesh['y2'=2,'y1'=2,'x'=4,'core'=2,'yhi'=2,'z3'=3,'za'=2,'zb'=2] {'y1','x..., dimensions={0} | all-to-all | bytes 524288 | tf_op jit(solution)/shard_map/all_to_all | solution.py:97
  54.6 0.1 reduce_sum.45
  54.7 25.6 %all_to_all.32 = bf16[12,16,256]{2,1,0:T(8,128)(2,1)S(1)} all-to-all(bf16[12,16,256]{2,1,0:T(8,128)(2,1)S(1)} %broadcast_in_dim.16), channel_id=1, replica_groups=mesh['y2'=2,'y1'=2,'x'=4,'core'=2,'yhi'=2,'z3'=3,'za'=2,'zb'=2] {'zb','z..., dimensions={0} | all-to-all | bytes 196608 | tf_op jit(solution)/shard_map/all_to_all | solution.py:89
  80.3 0.0 copy-start.2
  80.3 0.7 copy-done.2
  81.1 15.0 %all_to_all.33 = bf16[32,16,256]{2,1,0:T(8,128)(2,1)S(1)} all-to-all(bf16[32,16,256]{2,1,0:T(8,128)(2,1)S(1)} %broadcast_in_dim.17), channel_id=1, replica_groups=mesh['y2'=2,'y1'=2,'x'=4,'core'=2,'yhi'=2,'z3'=3,'za'=2,'zb'=2] {'y1','x..., dimensions={0} | all-to-all | bytes 524288 | tf_op jit(solution)/shard_map/all_to_all | solution.py:89
  96.1 0.4 convolution_convert_fusion
  96.5 2.4 %all-gather.3.both_ref = bf16[512,768]{1,0:T(8,128)(2,1)S(1)} all-gather(bf16[256,768]{1,0:T(8,128)(2,1)S(1)} %convolution_convert_fusion), channel_id=5, replica_groups=mesh['y2'=2,'y1'=2,'x'=4,'core'=2,'yhi'=2,'z3'=3,'za'=2,'zb'=2] {'core'}, dimensions={0}, use_global_device_ids=true | all-gather | bytes 1179648 | tf_op jit(solution)/shard_map/all_gather | solution.py:123
  98.8 0.7 tile.3
  99.6 2.4 %all-gather.4 = bf16[512,768]{1,0:T(8,128)(2,1)S(1)} all-gather(bf16[256,768]{1,0:T(8,128)(2,1)S(1)} %tile.3), channel_id=6, replica_groups=mesh['y2'=2,'y1'=2,'x'=4,'core'=2,'yhi'=2,'z3'=3,'za'=2,'zb'=2] {'core'}, dimensions={0}, use_global_device_ids=true | all-gather | bytes 1179648 | tf_op jit(solution)/shard_map/all_gather | solution.py:125
  101.9 0.4 convolution_convert_fusion.2
  102.4 12.9 %all_to_all.34 = bf16[16,32,256]{2,1,0:T(8,128)(2,1)S(1)} all-to-all(bf16[16,32,256]{2,1,0:T(8,128)(2,1)S(1)} %bitcast.32), channel_id=1, replica_groups=mesh['y2'=2,'y1'=2,'x'=4,'core'=2,'yhi'=2,'z3'=3,'za'=2,'zb'=2] {'y1','x..., dimensions={0} | all-to-all | bytes 524288 | tf_op jit(solution)/shard_map/all_to_all | solution.py:97
  115.3 16.2 %all_to_all.35 = bf16[12,32,256]{2,1,0:T(8,128)(2,1)S(1)} all-to-all(bf16[12,32,256]{2,1,0:T(8,128)(2,1)S(1)} %broadcast_in_dim.18), channel_id=1, replica_groups=mesh['y2'=2,'y1'=2,'x'=4,'core'=2,'yhi'=2,'z3'=3,'za'=2,'zb'=2] {'zb','z..., dimensions={0} | all-to-all | bytes 393216 | tf_op jit(solution)/shard_map/all_to_all | solution.py:89
  131.6 8.3 %all-gather.5 = bf16[64,256]{1,0:T(8,128)(2,1)S(1)} all-gather(bf16[32,256]{1,0:T(8,128)(2,1)S(1)} %reduce_sum.48), channel_id=7, replica_groups=mesh['y2'=2,'y1'=2,'x'=4,'core'=2,'yhi'=2,'z3'=3,'za'=2,'zb'=2] {'yhi'}, dimensions={0}, use_global_device_ids=true | all-gather | bytes 49152 | tf_op jit(solution)/shard_map/all_gather | solution.py:142
  139.9 0.6 fusion.9
  (7 shorter events, 0.2 us)
Async XLA Ops:
  29.3 2.5 %copy-start = (bf16[576,768]{1,0:T(8,128)(2,1)S(1)}, bf16[576,768]{1,0:T(8,128)(2,1)}, u32[]{:S(2)}) copy-start(bf16[576,768]{1,0:T(8,128)(2,1)} %screened_ref.3) | copy-start | bytes 2654212
  29.3 2.5 %copy-start.1 = (bf16[576,256]{1,0:T(8,128)(2,1)S(1)}, bf16[576,256]{1,0:T(8,128)(2,1)}, u32[]{:S(2)}) copy-start(bf16[576,256]{1,0:T(8,128)(2,1)} %val_ref.3) | copy-start | bytes 884740
  80.3 0.8 copy-start.2
